TPU v7x, 32 devices: a whole 2x2x4 slice. The times are simulated.
32 devices in a mesh: fsdp: 4 (over y, x), tensor: 8 (over z, core).
Axes of the slice: x: 2, y: 2, z: 4, core: 2. Of those that a mesh axis runs over, the one named last changes fastest.
Arguments:
- inputs_roll: bfloat16 [1536, 4096], P('fsdp', 'tensor'), may hold values from -6 to 6
- cotangent_roll: bfloat16 [1536, 4096], P('fsdp', 'tensor'), may hold values from -0.59765625 to 0.59765625
- counts: int32 [4, 4], P('fsdp'), may hold values from 1 to 3, as said below
- w_gate: bfloat16 [4096, 16384], P('fsdp', 'tensor'), may hold values from -0.09375 to 0.09375
- w_up: bfloat16 [4096, 16384], P('fsdp', 'tensor'), may hold values from -0.09375 to 0.09375
- w_down: bfloat16 [16384, 4096], P('tensor', 'fsdp'), may hold values from -0.046875 to 0.046875
Outputs:
- grad_inputs: bfloat16 [2304, 4096], P('fsdp', 'tensor')
- grad_gate: bfloat16 [4096, 16384], P('fsdp', 'tensor')
- grad_up: bfloat16 [4096, 16384], P('fsdp', 'tensor')
- grad_down: bfloat16 [16384, 4096], P('tensor', 'fsdp')
Inputs may be any that keep to these rules, and one draw needn't show every extreme that they name: Row s of counts splits rollout shard s's 8 blocks among the learner shards, in order of learner; every row sums to 8.
All inputs are finite; a program needn't handle non-finite values.
Results may differ from a plain program's by a relative error of at most 0.015.
Values may be sent and summed in bfloat16 or wider, within the bound.
No kernel may reach another device: no remote copies, remote signals or barrier semaphores. Data moves between devices by JAX's collectives and lax.ppermute only.
A program may use at most 128 MiB of HBM per device.

v0:
```python
import jax
import jax.numpy as jnp
from jax import lax
from jax.sharding import PartitionSpec as P


BLOCK = 48
MOST = 3


def swap(values, offset):
    size = lax.axis_size("fsdp")
    return lax.ppermute(values, "fsdp", [(i, i ^ offset) for i in range(size)])


class Grid:
    def __init__(self):
        self.n = lax.axis_size("fsdp")
        self.wide = lax.axis_size("tensor")
        self.m = self.wide // self.n
        assert self.n == 4 and self.wide % self.n == 0
        self.me = lax.axis_index("fsdp")
        here = lax.axis_index("tensor")
        self.line = here // self.m
        self.side = here % self.m

    def shift_line(self, values, r):
        n, m = self.n, self.m
        pairs = [(t, m * ((t // m + r) % n) + t % m) for t in range(self.wide)]
        return lax.ppermute(values, "tensor", pairs)

    def shift_side(self, values, r):
        m = self.m
        pairs = [(t, m * (t // m) + (t % m + r) % m) for t in range(self.wide)]
        return lax.ppermute(values, "tensor", pairs)


def matmul(left_side, right_side):
    return jnp.dot(left_side, right_side, preferred_element_type=jnp.float32)


def matmul_t(left_side, right_side):
    return lax.dot_general(
        left_side, right_side, (((1,), (1,)), ((), ())), preferred_element_type=jnp.float32
    )


def contract_rows(left_side, right_side):
    return lax.dot_general(
        left_side, right_side, (((0,), (0,)), ((), ())), preferred_element_type=jnp.float32
    )


def fence(*values):
    return lax.optimization_barrier(values)


def hand_out(grid, rows):
    n = grid.n
    quarters = rows.reshape(n, rows.shape[0] // n, rows.shape[1])
    turns = []
    for r in range(n):
        quarter = lax.dynamic_index_in_dim(quarters, (grid.line + r) % n, axis=0, keepdims=False)
        turns.append(grid.shift_line(quarter, r) if r else quarter)
    return turns


def to_learner_features(grid, turns):
    turns = jnp.stack(turns)
    piece = {}
    for k in range(grid.n):
        turn = (grid.line - (grid.me ^ k)) % grid.n
        piece[k] = lax.dynamic_index_in_dim(turns, turn, axis=0, keepdims=False)
        if k:
            piece[k] = swap(piece[k], k)
    return piece


def all_places(grid, mine):
    places = [mine] + [grid.shift_line(mine, r) for r in range(1, grid.n)]
    return jnp.stack(places, axis=1)


def all_sides(grid, half):
    m = grid.m
    width = half.shape[-1]
    sides = [half] + [grid.shift_side(half, r) for r in range(1, m)]
    blocks = []
    for i in range(half.shape[0]):
        columns = []
        for c in range(m):
            column = sides[0][i]
            for r in range(1, m):
                column = jnp.where((grid.side - c) % m == r, sides[r][i], column)
            columns.append(column.reshape(-1, width))
        blocks.append(jnp.concatenate(columns, axis=1))
    return blocks


def sum_over_tensor(grid, terms):
    n, m = grid.n, grid.m
    blocks, rows, depth = terms.shape
    half = depth // m

    def block(values, i, size):
        return lax.dynamic_slice_in_dim(values, i * size, size, axis=2)

    total = block(terms, grid.side, half).astype(jnp.float32)
    for r in range(1, m):
        sent = block(terms, (grid.side + r) % m, half)
        total = total + grid.shift_side(sent, r).astype(jnp.float32)
    total = low(total)
    width = half // n
    shape = (blocks, n, rows // n, width)
    kept = block(total, grid.line, width).astype(jnp.float32).reshape(shape)
    for r in range(1, n):
        sent = block(total, (grid.line + r) % n, width)
        came = grid.shift_line(sent, r).reshape(shape)
        kept = kept + jnp.roll(came, r, axis=1).astype(jnp.float32)
    return low(kept)


def route(grid, blocks, all_counts):
    n = grid.n
    width = blocks.shape[-1]
    per_place = blocks.shape[2] // BLOCK
    flat = blocks.reshape(-1, BLOCK, width)
    offsets = jnp.cumsum(all_counts, axis=1) - all_counts
    slot_ids = jnp.arange(MOST, dtype=jnp.int32)
    chosen = offsets.T[:, :, None] + slot_ids[None, None, :]
    is_live = slot_ids[None, None, :] < all_counts.T[:, :, None]
    shard = (grid.me ^ jnp.arange(n, dtype=jnp.int32))[None, :, None]
    place = (grid.line - chosen // per_place) % n
    index = (shard * n + place) * per_place + chosen % per_place
    index = jnp.where(is_live, index, 0)
    picked = jnp.take(flat, index.reshape(-1), axis=0)
    picked = picked.reshape(is_live.shape + (BLOCK, width))
    return jnp.where(is_live[:, :, :, None, None], picked, jnp.zeros_like(picked))


def return_rows(grid, sent):
    n = grid.n
    got = lax.all_to_all(sent, "fsdp", split_axis=0, concat_axis=0, tiled=True)
    turns = []
    for r in range(n):
        chunk = lax.dynamic_index_in_dim(got, (grid.line + r) % n, axis=0, keepdims=False)
        turns.append(grid.shift_line(chunk, r) if r else chunk)
    columns = []
    for q in range(n):
        column = turns[0]
        for r in range(1, n):
            column = jnp.where((grid.line - q) % n == r, turns[r], column)
        columns.append(column)
    return jnp.concatenate(columns, axis=1)


def low(values):
    return values.astype(jnp.bfloat16)


def plus(mine, came):
    return mine + came.astype(jnp.float32)


def steps(inputs_roll, cotangent_roll, counts, w_gate, w_up, w_down):
    grid = Grid()
    n = grid.n
    x, y = 1, 2

    def swap_x(values):
        return swap(values, x)

    def swap_y(values):
        return swap(values, y)

    turns = hand_out(grid, inputs_roll)
    *turns, cotangent_roll = fence(*turns, cotangent_roll)
    piece = to_learner_features(grid, turns)
    half3 = all_places(grid, piece[3][None])
    cot_turns = hand_out(grid, cotangent_roll)
    in3 = all_sides(grid, half3)[0]
    g3, u3 = low(matmul(in3, w_gate)), low(matmul(in3, w_up))

    g3_came, u3_came = swap_x(g3), swap_y(u3)
    half_others = all_places(grid, jnp.stack([piece[1], piece[2], piece[0]]))
    cot_piece = to_learner_features(grid, cot_turns)
    in1, in2, in0 = all_sides(grid, half_others)
    g1, u2 = low(matmul(in1, w_gate)), low(matmul(in2, w_up))

    g1_came, u2_came = swap_x(g1), swap_y(u2)
    cot_mine = jnp.stack([cot_piece[3], cot_piece[1], cot_piece[2], cot_piece[0]])
    cot_half = all_places(grid, cot_mine)
    g2, u1 = low(plus(matmul(in2, w_gate), g3_came)), low(plus(matmul(in1, w_up), u3_came))

    g2_came, u1_came = swap_y(g2), swap_x(u1)
    by_offset = jnp.concatenate([counts] + [swap(counts, k) for k in range(1, n)], axis=0)
    all_counts = jnp.take(by_offset, grid.me ^ jnp.arange(n, dtype=jnp.int32), axis=0)
    g0, u0 = matmul(in0, w_gate), matmul(in0, w_up)
    cot3, cot1, cot2, cot0 = all_sides(grid, cot_half)
    cut = cot3.shape[0] // 2
    h3a, h3b = low(matmul_t(cot3[:cut], w_down)), low(matmul_t(cot3[cut:], w_down))
    h1a, h2b = low(matmul_t(cot1[:cut], w_down)), low(matmul_t(cot2[cut:], w_down))
    g1_came, u2_came, h3a, h3b, h1a, h2b = fence(g1_came, u2_came, h3a, h3b, h1a, h2b)

    h3a_came, h3b_came = swap_x(h3a), swap_y(h3b)
    h1a_came, h2b_came = swap_x(h1a), swap_y(h2b)
    h2a, h1b = matmul_t(cot2[:cut], w_down), matmul_t(cot1[cut:], w_down)
    h0 = matmul_t(cot0, w_down)

    gate_act = plus(plus(g0, g1_came), g2_came)
    up_act = plus(plus(u0, u2_came), u1_came)
    sigmoid_gate = jax.nn.sigmoid(gate_act)
    silu_gate = gate_act * sigmoid_gate
    hidden = low(silu_gate * up_act)
    hidden1, hidden2 = swap_x(hidden), swap_y(hidden)

    h2a_came = swap_y(low(plus(h2a, h3a_came)))
    h1b_came = swap_x(low(plus(h1b, h3b_came)))

    h2a_came, h1b_came, hidden1, hidden2 = fence(h2a_came, h1b_came, hidden1, hidden2)
    hidden3a, hidden3b = swap_x(hidden2[:cut]), swap_y(hidden1[cut:])

    h_first = jnp.concatenate([h1a_came, h1b_came], axis=0)
    h_second = jnp.concatenate([h2a_came, h2b_came], axis=0)
    grad_hidden = plus(plus(h0, h_first), h_second)
    gate0 = low(grad_hidden * up_act * sigmoid_gate * (1.0 + gate_act * (1.0 - sigmoid_gate)))
    up0 = low(grad_hidden * silu_gate)
    gate0, up0 = fence(gate0, up0)
    up1, up2 = swap_x(up0), swap_y(up0)

    def input_terms(up_block, gate_block):
        return low(matmul_t(up_block, w_up) + matmul_t(gate_block, w_gate))

    hidden3 = jnp.concatenate([hidden3a, hidden3b], axis=0)
    hidden3, gate0, up0 = fence(hidden3, gate0, up0)
    gate1, gate2 = swap_x(gate0), swap_y(gate0)
    terms0 = input_terms(up0, gate0)
    terms0 = sum_over_tensor(grid, terms0[None])
    rows_in = jnp.concatenate([in0, in1, in2, in3], axis=0)
    rows_cot = jnp.concatenate([cot0, cot1, cot2, cot3], axis=0)
    all_hidden = jnp.concatenate([hidden, hidden1, hidden2, hidden3], axis=0)
    grad_down = low(contract_rows(all_hidden, rows_cot))

    up3a, up3b = swap_x(up2[:cut]), swap_y(up1[cut:])
    up_terms1, up_terms2 = matmul_t(up1, w_up), matmul_t(up2, w_up)
    up_terms1, up_terms2 = fence(up_terms1, up_terms2)
    terms1 = low(up_terms1 + matmul_t(gate1, w_gate))
    terms2 = low(up_terms2 + matmul_t(gate2, w_gate))
    terms12 = sum_over_tensor(grid, jnp.stack([terms1, terms2]))

    gate3a, gate3b = swap_x(gate2[:cut]), swap_y(gate1[cut:])
    (up3,) = fence(jnp.concatenate([up3a, up3b], axis=0))
    grad_up = low(contract_rows(rows_in, jnp.concatenate([up0, up1, up2, up3], axis=0)))

    gate3 = jnp.concatenate([gate3a, gate3b], axis=0)
    (gate3,) = fence(gate3)
    terms3 = sum_over_tensor(grid, input_terms(up3, gate3)[None])
    all_gate = jnp.concatenate([gate0, gate1, gate2, gate3], axis=0)
    grad_gate = low(contract_rows(rows_in, all_gate))
    sent = route(grid, jnp.concatenate([terms0, terms12, terms3], axis=0), all_counts)
    grad_inputs = return_rows(grid, sent.reshape(n, -1, sent.shape[-1]))
    return (grad_inputs, grad_gate, grad_up, grad_down)


def solution(mesh):
    return jax.shard_map(
        steps,
        mesh=mesh,
        in_specs=(
            P("fsdp", "tensor"),
            P("fsdp", "tensor"),
            P("fsdp", None),
            P("fsdp", "tensor"),
            P("fsdp", "tensor"),
            P("tensor", "fsdp"),
        ),
        out_specs=(
            P("fsdp", "tensor"),
            P("fsdp", "tensor"),
            P("fsdp", "tensor"),
            P("tensor", "fsdp"),
        ),
        check_vma=False,
    )
```

profile of v0, /device:TPU:0, one launch (start us, length us, event | category | flops | bytes accessed | tf_op | source)
XLA Modules:
  0.0 482.7 jit_solution(8634643775587662287)
XLA Ops:
  1.8 3.1 collective-permute-start.3
  4.9 2.6 collective-permute-start.4
  10.6 3.5 collective-permute-done.4
  14.2 2.5 collective-permute-start.28
  18.8 2.6 collective-permute-start.6
  26.5 1.8 collective-permute-start.31
  28.3 3.9 collective-permute-done.7
  32.6 12.0 %collective-permute-start.19 = (bf16[3,96,512]{2,1,0:T(8,128)(2,1)S(1)}, bf16[3,96,512]{2,1,0:T(8,128)(2,1)S(1)}, u32[]{:S(2)}, u32[]{:S(2)}) collective-permute-start(bf16[3,96,512]{2,1,0:T(8,128)(2,1)S(1)} %get-tuple-element.104), channel_id=1, source_target_pairs={{0,4},{1,5},{2,6},{3,7},{4,0},{5,1},{6,2},{7,3},{8,12},{9,13},{10,... | collective-permute-start | bytes 884744 | tf_op jit(solution)/shard_map/ppermute | solution.py:30
  44.6 3.6 collective-permute-start.20
  48.2 2.4 collective-permute-start.9
  51.3 2.5 collective-permute-done.9
  55.8 4.1 collective-permute-done.11
  60.7 7.0 %collective-permute-start.14 = (bf16[4,96,512]{2,1,0:T(8,128)(2,1)S(1)}, bf16[4,96,512]{2,1,0:T(8,128)(2,1)S(1)}, u32[]{:S(2)}, u32[]{:S(2)}) collective-permute-start(bf16[4,96,512]{2,1,0:T(8,128)(2,1)S(1)} %get-tuple-element.90), channel_id=1, source_target_pairs={{0,6},{1,7},{2,0},{3,1},{4,2},{5,3},{6,4},{7,5},{8,14},{9,15},{10,... | collective-permute-start | bytes 1179656 | tf_op jit(solution)/shard_map/ppermute | solution.py:30
  68.1 1.8 convolution_convert_fusion.1
  71.5 1.8 convolution_convert_fusion
  74.9 15.5 %collective-permute-done.13 = bf16[4,96,512]{2,1,0:T(8,128)(2,1)S(1)} collective-permute-done((bf16[4,96,512]{2,1,0:T(8,128)(2,1)S(1)}, bf16[4,96,512]{2,1,0:T(8,128)(2,1)S(1)}, u32[]{:S(2)}, u32[]{:S(2)}) %collective-permute-start.13) | collective-permute-done | bytes 393248 | tf_op jit(solution)/shard_map/ppermute | solution.py:30
  97.7 9.6 %collective-permute-done.33 = bf16[384,2048]{1,0:T(8,128)(2,1)S(1)} collective-permute-done((bf16[384,2048]{1,0:T(8,128)(2,1)S(1)}, bf16[384,2048]{1,0:T(8,128)(2,1)S(1)}, u32[]{:S(2)}, u32[]{:S(2)}) %collective-permute-start.33) | collective-permute-done | bytes 1572896 | tf_op jit(solution)/shard_map/ppermute | solution.py:13
  111.2 1.8 add_convert_fusion
  116.8 2.4 convolution_convert_fusion.7
  119.3 2.0 convolution_convert_fusion.4
  121.2 2.4 convolution_convert_fusion.5
  123.7 21.2 %collective-permute-done.23 = bf16[384,2048]{1,0:T(8,128)(2,1)S(1)} collective-permute-done((bf16[384,2048]{1,0:T(8,128)(2,1)S(1)}, bf16[384,2048]{1,0:T(8,128)(2,1)S(1)}, u32[]{:S(2)}, u32[]{:S(2)}) %collective-permute-start.23) | collective-permute-done | bytes 1572896 | tf_op jit(solution)/shard_map/ppermute | solution.py:13
  150.4 43.8 %collective-permute-done.26 = bf16[192,2048]{1,0:T(8,128)(2,1)S(1)} collective-permute-done((bf16[192,2048]{1,0:T(8,128)(2,1)S(1)}, bf16[192,2048]{1,0:T(8,128)(2,1)S(1)}, u32[]{:S(2)}, u32[]{:S(2)}) %collective-permute-start.26) | collective-permute-done | bytes 786464 | tf_op jit(solution)/shard_map/ppermute | solution.py:13
  194.2 2.4 add_convert_fusion.7
  197.5 4.6 multiply_convert_fusion.2
  206.6 31.9 %collective-permute-done.1 = s32[1,4]{1,0:T(1,128)S(1)} collective-permute-done((s32[1,4]{1,0:T(1,128)}, s32[1,4]{1,0:T(1,128)S(1)}, u32[]{:S(2)}, u32[]{:S(2)}) %collective-permute-start.1) | collective-permute-done | bytes 48 | tf_op jit(solution)/shard_map/ppermute | solution.py:13
  240.2 10.1 %collective-permute-done.2 = s32[1,4]{1,0:T(1,128)S(1)} collective-permute-done((s32[1,4]{1,0:T(1,128)}, s32[1,4]{1,0:T(1,128)S(1)}, u32[]{:S(2)}, u32[]{:S(2)}) %collective-permute-start.2) | collective-permute-done | bytes 48 | tf_op jit(solution)/shard_map/ppermute | solution.py:13
  252.2 4.6 add_convert_fusion.8
  256.8 2.1 collective-permute-start.25
  260.7 25.6 %collective-permute-done.25 = bf16[192,2048]{1,0:T(8,128)(2,1)} collective-permute-done((bf16[192,2048]{1,0:T(8,128)(2,1)}, bf16[192,2048]{1,0:T(8,128)(2,1)}, u32[]{:S(2)}, u32[]{:S(2)}) %collective-permute-start.25) | collective-permute-done | bytes 786464 | tf_op jit(solution)/shard_map/ppermute | solution.py:13
  290.8 11.0 %multiply_convert_fusion = (bf16[384,2048]{1,0:T(8,128)(2,1)}, bf16[384,2048]{1,0:T(8,128)(2,1)S(1)}) fusion(bf16[384,2048]{1,0:T(8,128)(2,1)} %copy-done.39, f32[384,2048]{1,0:T(8,128)} %copy-done.41, bf16[384,2048]{1,0:T(8,128)(2,1)} %copy-done.38, bf16[384,2048]{1,0:T(8,128)(2,1)} %copy-done.40, f32[384,2048]{1,0:T(8,128)} %get-tuple-element.114, ...), kind=kOutput, calls=%fused_computation.45 | convolution fusion | flops 1636564992 | bytes 23855104 | tf_op jit(solution)/shard_map/dot_general | solution.py:43
  301.9 1.8 collective-permute-start.48
  304.0 1.9 collective-permute-done.39
  306.0 4.9 %collective-permute-done.40 = bf16[192,2048]{1,0:T(8,128)(2,1)S(1)} collective-permute-done((bf16[192,2048]{1,0:T(8,128)(2,1)S(1)}, bf16[192,2048]{1,0:T(8,128)(2,1)S(1)}, u32[]{:S(2)}, u32[]{:S(2)}) %collective-permute-start.40) | collective-permute-done | bytes 786464 | tf_op jit(solution)/shard_map/ppermute | solution.py:13
  311.0 1.8 fusion.134
  313.2 3.4 add_convert_fusion.6
  325.0 10.5 %collective-permute-start.44 = (bf16[1,384,128]{2,1,0:T(8,128)(2,1)S(1)}, bf16[1,384,128]{2,1,0:T(8,128)(2,1)S(1)}, u32[]{:S(2)}, u32[]{:S(2)}) collective-permute-start(bf16[1,384,128]{2,1,0:T(8,128)(2,1)S(1)} %get-tuple-element.79), channel_id=1, source_target_pairs={{0,2},{1,3},{2,4},{3,5},{4,6},{5,7},{6,0},{7,1},{8,10},{9,11},{10,... | collective-permute-start | bytes 294920 | tf_op jit(solution)/shard_map/ppermute | solution.py:30
  335.6 9.2 %collective-permute-done.48 = bf16[384,2048]{1,0:T(8,128)(2,1)} collective-permute-done((bf16[384,2048]{1,0:T(8,128)(2,1)}, bf16[384,2048]{1,0:T(8,128)(2,1)}, u32[]{:S(2)}, u32[]{:S(2)}) %collective-permute-start.48) | collective-permute-done | bytes 1572896 | tf_op jit(solution)/shard_map/ppermute | solution.py:13
  345.2 4.7 fusion.136
  350.0 2.1 slice.238
  353.5 3.4 fusion.135
  356.9 2.1 slice.239
  359.0 16.4 %collective-permute-done.50 = bf16[384,2048]{1,0:T(8,128)(2,1)} collective-permute-done((bf16[384,2048]{1,0:T(8,128)(2,1)}, bf16[384,2048]{1,0:T(8,128)(2,1)}, u32[]{:S(2)}, u32[]{:S(2)}) %collective-permute-start.50) | collective-permute-done | bytes 1572896 | tf_op jit(solution)/shard_map/ppermute | solution.py:13
  375.7 2.1 slice.240
  377.8 3.2 fusion.138
  381.8 1.8 fusion.137
  385.1 1.8 collective-permute-start.58
  387.5 11.4 %fusion.24 = bf16[2048,1024]{1,0:T(8,128)(2,1)} fusion(bf16[384,2048]{1,0:T(8,128)(2,1)S(1)} %pad_maximum_fusion.1, bf16[384,2048]{1,0:T(8,128)(2,1)} %collective-permute-done.38, bf16[384,2048]{1,0:T(8,128)(2,1)} %collective-permute-done.37, bf16[384,2048]{1,0:T(8,128)(2,1)} %get-tuple-element.113, bf16[384,512]{1,0:T(8,128)(2,1)S(1)} %bitcast.189, ...), kind=kOutput, calls=%fused_computation.26 | convolution fusion | flops 6494879744 | bytes 13631488 | tf_op jit(solution)/shard_map/dot_general | solution.py:49
  402.3 8.5 %collective-permute-start.45 = (bf16[1,384,128]{2,1,0:T(8,128)(2,1)}, bf16[1,384,128]{2,1,0:T(8,128)(2,1)S(1)}, u32[]{:S(2)}, u32[]{:S(2)}) collective-permute-start(bf16[1,384,128]{2,1,0:T(8,128)(2,1)} %get-tuple-element.78), channel_id=1, source_target_pairs={{0,4},{1,5},{2,6},{3,7},{4,0},{5,1},{6,2},{7,3},{8,12},{9,13},{10,... | collective-permute-start | bytes 294920 | tf_op jit(solution)/shard_map/ppermute | solution.py:30
  412.4 2.0 pad_maximum_fusion.3
  416.2 2.3 collective-permute-start.53
  418.4 3.0 collective-permute-start.52
  421.4 1.8 collective-permute-start.54
  423.3 1.8 fusion.139
  425.1 1.9 add_convert_fusion.2
  427.1 5.4 %collective-permute-done.52 = bf16[2,384,128]{2,1,0:T(8,128)(2,1)S(1)} collective-permute-done((bf16[2,384,128]{2,1,0:T(8,128)(2,1)S(1)}, bf16[2,384,128]{2,1,0:T(8,128)(2,1)S(1)}, u32[]{:S(2)}, u32[]{:S(2)}) %collective-permute-start.52) | collective-permute-done | bytes 196640 | tf_op jit(solution)/shard_map/ppermute | solution.py:30
  434.5 3.6 collective-permute-start.61
  438.1 3.8 collective-permute-start.62
  442.1 3.5 collective-permute-done.60
  446.9 2.0 fusion.61
  448.8 3.7 all-to-all-start
  452.6 12.3 %fusion.27 = bf16[1024,2048]{1,0:T(8,128)(2,1)} fusion(bf16[384,2048]{1,0:T(8,128)(2,1)} %copy-done.1, bf16[384,2048]{1,0:T(8,128)(2,1)} %collective-permute-done.48, bf16[384,2048]{1,0:T(8,128)(2,1)} %collective-permute-done.47, bf16[384,2048]{1,0:T(8,128)(2,1)} %get-tuple-element.43, bf16[384,512]{1,0:T(8,128)(2,1)} %bitcast.236, ...), kind=kOutput, calls=%fused_computation.27 | convolution fusion | flops 6494879744 | bytes 13631488 | tf_op jit(solution)/shard_map/dot_general | solution.py:49
  465.0 3.0 collective-permute-start.63
  469.5 11.7 %fusion.30 = bf16[1024,2048]{1,0:T(8,128)(2,1)} fusion(bf16[384,2048]{1,0:T(8,128)(2,1)S(1)} %pad_maximum_fusion.3, bf16[384,2048]{1,0:T(8,128)(2,1)} %collective-permute-done.50, bf16[384,2048]{1,0:T(8,128)(2,1)} %copy-done.14, bf16[384,2048]{1,0:T(8,128)(2,1)} %copy-done.35, bf16[384,512]{1,0:T(8,128)(2,1)} %bitcast.237, bf16[384,512]{1,0:T(8,128)(2,1)} %bitcast.233, ...), kind=kOutput, calls=%fused_computation.28 | convolution fusion | flops 6494879744 | bytes 13631488 | tf_op jit(solution)/shard_map/dot_general | solution.py:49
  (261 shorter events, 81.2 us)
Async XLA Ops:
  1.8 8.8 %collective-permute-start.3 = (bf16[96,512]{1,0:T(8,128)(2,1)S(1)}, bf16[96,512]{1,0:T(8,128)(2,1)S(1)}, u32[]{:S(2)}, u32[]{:S(2)}) collective-permute-start(bf16[96,512]{1,0:T(8,128)(2,1)S(1)} %get-tuple-element.101), channel_id=1, source_target_pairs={{0,2},{1,3},{2,4},{3,5},{4,6},{5,7},{6,0},{7,1},{8,10},{9,11},{10,... | collective-permute-start | bytes 294920 | tf_op jit(solution)/shard_map/ppermute | solution.py:30
  4.9 9.2 %collective-permute-start.4 = (bf16[96,512]{1,0:T(8,128)(2,1)S(1)}, bf16[96,512]{1,0:T(8,128)(2,1)S(1)}, u32[]{:S(2)}, u32[]{:S(2)}) collective-permute-start(bf16[96,512]{1,0:T(8,128)(2,1)S(1)} %get-tuple-element.100), channel_id=1, source_target_pairs={{0,4},{1,5},{2,6},{3,7},{4,0},{5,1},{6,2},{7,3},{8,12},{9,13},{10,... | collective-permute-start | bytes 294920 | tf_op jit(solution)/shard_map/ppermute | solution.py:30
  7.5 6.6 %collective-permute-start.5 = (bf16[96,512]{1,0:T(8,128)(2,1)S(1)}, bf16[96,512]{1,0:T(8,128)(2,1)S(1)}, u32[]{:S(2)}, u32[]{:S(2)}) collective-permute-start(bf16[96,512]{1,0:T(8,128)(2,1)S(1)} %get-tuple-element.99), channel_id=1, source_target_pairs={{0,6},{1,7},{2,0},{3,1},{4,2},{5,3},{6,4},{7,5},{8,14},{9,15},{10,... | collective-permute-start | bytes 294920 | tf_op jit(solution)/shard_map/ppermute | solution.py:30
  14.2 8.8 %collective-permute-start.28 = (bf16[96,512]{1,0:T(8,128)(2,1)S(1)}, bf16[96,512]{1,0:T(8,128)(2,1)S(1)}, u32[]{:S(2)}, u32[]{:S(2)}) collective-permute-start(bf16[96,512]{1,0:T(8,128)(2,1)S(1)} %get-tuple-element.85), channel_id=1, source_target_pairs={{0,24},{8,16},{16,8},{24,0},{1,25},{9,17},{17,9},{25,1},{2,26},{10... | collective-permute-start | bytes 294920 | tf_op jit(solution)/shard_map/ppermute | solution.py:13
  16.7 7.1 %collective-permute-start.16 = (bf16[96,512]{1,0:T(8,128)(2,1)S(1)}, bf16[96,512]{1,0:T(8,128)(2,1)S(1)}, u32[]{:S(2)}, u32[]{:S(2)}) collective-permute-start(bf16[96,512]{1,0:T(8,128)(2,1)S(1)} %get-tuple-element.88), channel_id=1, source_target_pairs={{0,8},{8,0},{16,24},{24,16},{1,9},{9,1},{17,25},{25,17},{2,10},{10... | collective-permute-start | bytes 294920 | tf_op jit(solution)/shard_map/ppermute | solution.py:13
  17.3 7.8 %collective-permute-start.17 = (bf16[96,512]{1,0:T(8,128)(2,1)S(1)}, bf16[96,512]{1,0:T(8,128)(2,1)S(1)}, u32[]{:S(2)}, u32[]{:S(2)}) collective-permute-start(bf16[96,512]{1,0:T(8,128)(2,1)S(1)} %get-tuple-element.87), channel_id=1, source_target_pairs={{0,16},{8,24},{16,0},{24,8},{1,17},{9,25},{17,1},{25,9},{2,18},{10... | collective-permute-start | bytes 294920 | tf_op jit(solution)/shard_map/ppermute | solution.py:13
  18.8 7.6 %collective-permute-start.6 = (bf16[96,512]{1,0:T(8,128)(2,1)S(1)}, bf16[96,512]{1,0:T(8,128)(2,1)S(1)}, u32[]{:S(2)}, u32[]{:S(2)}) collective-permute-start(bf16[96,512]{1,0:T(8,128)(2,1)S(1)} %get-tuple-element.98), channel_id=1, source_target_pairs={{0,2},{1,3},{2,4},{3,5},{4,6},{5,7},{6,0},{7,1},{8,10},{9,11},{10,... | collective-permute-start | bytes 294920 | tf_op jit(solution)/shard_map/ppermute | solution.py:30
  21.4 10.8 %collective-permute-start.7 = (bf16[96,512]{1,0:T(8,128)(2,1)S(1)}, bf16[96,512]{1,0:T(8,128)(2,1)S(1)}, u32[]{:S(2)}, u32[]{:S(2)}) collective-permute-start(bf16[96,512]{1,0:T(8,128)(2,1)S(1)} %get-tuple-element.97), channel_id=1, source_target_pairs={{0,4},{1,5},{2,6},{3,7},{4,0},{5,1},{6,2},{7,3},{8,12},{9,13},{10,... | collective-permute-start | bytes 294920 | tf_op jit(solution)/shard_map/ppermute | solution.py:30
  23.1 9.5 %collective-permute-start.8 = (bf16[96,512]{1,0:T(8,128)(2,1)S(1)}, bf16[96,512]{1,0:T(8,128)(2,1)S(1)}, u32[]{:S(2)}, u32[]{:S(2)}) collective-permute-start(bf16[96,512]{1,0:T(8,128)(2,1)S(1)} %get-tuple-element.96), channel_id=1, source_target_pairs={{0,6},{1,7},{2,0},{3,1},{4,2},{5,3},{6,4},{7,5},{8,14},{9,15},{10,... | collective-permute-start | bytes 294920 | tf_op jit(solution)/shard_map/ppermute | solution.py:30
  23.9 20.8 %collective-permute-start.29 = (bf16[1,96,512]{2,1,0:T(8,128)(2,1)S(1)}, bf16[1,96,512]{2,1,0:T(8,128)(2,1)S(1)}, u32[]{:S(2)}, u32[]{:S(2)}) collective-permute-start(bf16[1,96,512]{2,1,0:T(8,128)(2,1)S(1)} %bitcast.239), channel_id=1, source_target_pairs={{0,2},{1,3},{2,4},{3,5},{4,6},{5,7},{6,0},{7,1},{8,10},{9,11},{10,... | collective-permute-start | bytes 294920 | tf_op jit(solution)/shard_map/ppermute | solution.py:30
  25.1 23.1 %collective-permute-start.30 = (bf16[1,96,512]{2,1,0:T(8,128)(2,1)S(1)}, bf16[1,96,512]{2,1,0:T(8,128)(2,1)S(1)}, u32[]{:S(2)}, u32[]{:S(2)}) collective-permute-start(bf16[1,96,512]{2,1,0:T(8,128)(2,1)S(1)} %bitcast.240), channel_id=1, source_target_pairs={{0,4},{1,5},{2,6},{3,7},{4,0},{5,1},{6,2},{7,3},{8,12},{9,13},{10,... | collective-permute-start | bytes 294920 | tf_op jit(solution)/shard_map/ppermute | solution.py:30
  26.5 24.2 %collective-permute-start.31 = (bf16[1,96,512]{2,1,0:T(8,128)(2,1)S(1)}, bf16[1,96,512]{2,1,0:T(8,128)(2,1)S(1)}, u32[]{:S(2)}, u32[]{:S(2)}) collective-permute-start(bf16[1,96,512]{2,1,0:T(8,128)(2,1)S(1)} %bitcast.241), channel_id=1, source_target_pairs={{0,6},{1,7},{2,0},{3,1},{4,2},{5,3},{6,4},{7,5},{8,14},{9,15},{10,... | collective-permute-start | bytes 294920 | tf_op jit(solution)/shard_map/ppermute | solution.py:30
  32.2 27.8 %collective-permute-start.18 = (bf16[3,96,512]{2,1,0:T(8,128)(2,1)S(1)}, bf16[3,96,512]{2,1,0:T(8,128)(2,1)S(1)}, u32[]{:S(2)}, u32[]{:S(2)}) collective-permute-start(bf16[3,96,512]{2,1,0:T(8,128)(2,1)S(1)} %get-tuple-element.104), channel_id=1, source_target_pairs={{0,2},{1,3},{2,4},{3,5},{4,6},{5,7},{6,0},{7,1},{8,10},{9,11},{10,... | collective-permute-start | bytes 884744 | tf_op jit(solution)/shard_map/ppermute | solution.py:30
  32.6 28.1 %collective-permute-start.19 = (bf16[3,96,512]{2,1,0:T(8,128)(2,1)S(1)}, bf16[3,96,512]{2,1,0:T(8,128)(2,1)S(1)}, u32[]{:S(2)}, u32[]{:S(2)}) collective-permute-start(bf16[3,96,512]{2,1,0:T(8,128)(2,1)S(1)} %get-tuple-element.104), channel_id=1, source_target_pairs={{0,4},{1,5},{2,6},{3,7},{4,0},{5,1},{6,2},{7,3},{8,12},{9,13},{10,... | collective-permute-start | bytes 884744 | tf_op jit(solution)/shard_map/ppermute | solution.py:30
  44.6 23.1 %collective-permute-start.20 = (bf16[3,96,512]{2,1,0:T(8,128)(2,1)S(1)}, bf16[3,96,512]{2,1,0:T(8,128)(2,1)S(1)}, u32[]{:S(2)}, u32[]{:S(2)}) collective-permute-start(bf16[3,96,512]{2,1,0:T(8,128)(2,1)S(1)} %get-tuple-element.104), channel_id=1, source_target_pairs={{0,6},{1,7},{2,0},{3,1},{4,2},{5,3},{6,4},{7,5},{8,14},{9,15},{10,... | collective-permute-start | bytes 884744 | tf_op jit(solution)/shard_map/ppermute | solution.py:30
  48.2 5.5 %collective-permute-start.9 = (bf16[96,512]{1,0:T(8,128)(2,1)S(1)}, bf16[96,512]{1,0:T(8,128)(2,1)S(1)}, u32[]{:S(2)}, u32[]{:S(2)}) collective-permute-start(bf16[96,512]{1,0:T(8,128)(2,1)S(1)} %get-tuple-element.91), channel_id=1, source_target_pairs={{0,24},{8,16},{16,8},{24,0},{1,25},{9,17},{17,9},{25,1},{2,26},{10... | collective-permute-start | bytes 294920 | tf_op jit(solution)/shard_map/ppermute | solution.py:13
  53.7 14.2 %collective-permute-start.32 = (bf16[1,4,96,512]{3,2,0,1:T(8,128)(2,1)S(1)}, bf16[1,4,96,512]{3,2,0,1:T(8,128)(2,1)S(1)}, u32[]{:S(2)}, u32[]{:S(2)}) collective-permute-start(bf16[1,4,96,512]{3,2,0,1:T(8,128)(2,1)S(1)} %pad_maximum_fusion.33), channel_id=1, source_target_pairs={{0,1},{1,0},{2,3},{3,2},{4,5},{5,4},{6,7},{7,6},{8,9},{9,8},{10,11... | collective-permute-start | bytes 1179656 | tf_op jit(solution)/shard_map/ppermute | solution.py:35
  60.0 13.9 %collective-permute-start.12 = (bf16[4,96,512]{2,1,0:T(8,128)(2,1)S(1)}, bf16[4,96,512]{2,1,0:T(8,128)(2,1)S(1)}, u32[]{:S(2)}, u32[]{:S(2)}) collective-permute-start(bf16[4,96,512]{2,1,0:T(8,128)(2,1)S(1)} %get-tuple-element.90), channel_id=1, source_target_pairs={{0,2},{1,3},{2,4},{3,5},{4,6},{5,7},{6,0},{7,1},{8,10},{9,11},{10,... | collective-permute-start | bytes 1179656 | tf_op jit(solution)/shard_map/ppermute | solution.py:30
  60.1 30.4 %collective-permute-start.13 = (bf16[4,96,512]{2,1,0:T(8,128)(2,1)S(1)}, bf16[4,96,512]{2,1,0:T(8,128)(2,1)S(1)}, u32[]{:S(2)}, u32[]{:S(2)}) collective-permute-start(bf16[4,96,512]{2,1,0:T(8,128)(2,1)S(1)} %get-tuple-element.90), channel_id=1, source_target_pairs={{0,4},{1,5},{2,6},{3,7},{4,0},{5,1},{6,2},{7,3},{8,12},{9,13},{10,... | collective-permute-start | bytes 1179656 | tf_op jit(solution)/shard_map/ppermute | solution.py:30
  60.7 29.7 %collective-permute-start.14 = (bf16[4,96,512]{2,1,0:T(8,128)(2,1)S(1)}, bf16[4,96,512]{2,1,0:T(8,128)(2,1)S(1)}, u32[]{:S(2)}, u32[]{:S(2)}) collective-permute-start(bf16[4,96,512]{2,1,0:T(8,128)(2,1)S(1)} %get-tuple-element.90), channel_id=1, source_target_pairs={{0,6},{1,7},{2,0},{3,1},{4,2},{5,3},{6,4},{7,5},{8,14},{9,15},{10,... | collective-permute-start | bytes 1179656 | tf_op jit(solution)/shard_map/ppermute | solution.py:30
  67.9 22.8 %collective-permute-start.21 = (bf16[3,4,96,512]{3,2,0,1:T(8,128)(2,1)S(1)}, bf16[3,4,96,512]{3,2,0,1:T(8,128)(2,1)S(1)}, u32[]{:S(2)}, u32[]{:S(2)}) collective-permute-start(bf16[3,4,96,512]{3,2,0,1:T(8,128)(2,1)S(1)} %pad_maximum_fusion.4), channel_id=1, source_target_pairs={{0,1},{1,0},{2,3},{3,2},{4,5},{5,4},{6,7},{7,6},{8,9},{9,8},{10,11... | collective-permute-start | bytes 3538952 | tf_op jit(solution)/shard_map/ppermute | solution.py:35
  69.9 37.3 %collective-permute-start.33 = (bf16[384,2048]{1,0:T(8,128)(2,1)S(1)}, bf16[384,2048]{1,0:T(8,128)(2,1)S(1)}, u32[]{:S(2)}, u32[]{:S(2)}) collective-permute-start(bf16[384,2048]{1,0:T(8,128)(2,1)S(1)} %convolution_convert_fusion.1), channel_id=1, source_target_pairs={{0,8},{8,0},{16,24},{24,16},{1,9},{9,1},{17,25},{25,17},{2,10},{10... | collective-permute-start | bytes 4718600 | tf_op jit(solution)/shard_map/ppermute | solution.py:13
  73.9 37.3 %collective-permute-start.35 = (bf16[384,2048]{1,0:T(8,128)(2,1)S(1)}, bf16[384,2048]{1,0:T(8,128)(2,1)S(1)}, u32[]{:S(2)}, u32[]{:S(2)}) collective-permute-start(bf16[384,2048]{1,0:T(8,128)(2,1)S(1)} %convolution_convert_fusion), channel_id=1, source_target_pairs={{0,16},{8,24},{16,0},{24,8},{1,17},{9,25},{17,1},{25,9},{2,18},{10... | collective-permute-start | bytes 4718600 | tf_op jit(solution)/shard_map/ppermute | solution.py:13
  90.6 23.5 %collective-permute-start.15 = (bf16[4,4,96,512]{3,2,0,1:T(8,128)(2,1)S(1)}, bf16[4,4,96,512]{3,2,0,1:T(8,128)(2,1)S(1)}, u32[]{:S(2)}, u32[]{:S(2)}) collective-permute-start(bf16[4,4,96,512]{3,2,0,1:T(8,128)(2,1)S(1)} %pad_maximum_fusion), channel_id=1, source_target_pairs={{0,1},{1,0},{2,3},{3,2},{4,5},{5,4},{6,7},{7,6},{8,9},{9,8},{10,11... | collective-permute-start | bytes 4718600 | tf_op jit(solution)/shard_map/ppermute | solution.py:35
  92.7 52.1 %collective-permute-start.23 = (bf16[384,2048]{1,0:T(8,128)(2,1)S(1)}, bf16[384,2048]{1,0:T(8,128)(2,1)S(1)}, u32[]{:S(2)}, u32[]{:S(2)}) collective-permute-start(bf16[384,2048]{1,0:T(8,128)(2,1)S(1)} %convolution_convert_fusion.2), channel_id=1, source_target_pairs={{0,16},{8,24},{16,0},{24,8},{1,17},{9,25},{17,1},{25,9},{2,18},{10... | collective-permute-start | bytes 4718600 | tf_op jit(solution)/shard_map/ppermute | solution.py:13
  96.1 48.8 %collective-permute-start.22 = (bf16[384,2048]{1,0:T(8,128)(2,1)S(1)}, bf16[384,2048]{1,0:T(8,128)(2,1)S(1)}, u32[]{:S(2)}, u32[]{:S(2)}) collective-permute-start(bf16[384,2048]{1,0:T(8,128)(2,1)S(1)} %convolution_convert_fusion.3), channel_id=1, source_target_pairs={{0,8},{8,0},{16,24},{24,16},{1,9},{9,1},{17,25},{25,17},{2,10},{10... | collective-permute-start | bytes 4718600 | tf_op jit(solution)/shard_map/ppermute | solution.py:13
  109.1 88.4 %collective-permute-start.34 = (bf16[384,2048]{1,0:T(8,128)(2,1)S(1)}, bf16[384,2048]{1,0:T(8,128)(2,1)S(1)}, u32[]{:S(2)}, u32[]{:S(2)}) collective-permute-start(bf16[384,2048]{1,0:T(8,128)(2,1)S(1)} %add_convert_fusion.1), channel_id=1, source_target_pairs={{0,16},{8,24},{16,0},{24,8},{1,17},{9,25},{17,1},{25,9},{2,18},{10... | collective-permute-start | bytes 4718600 | tf_op jit(solution)/shard_map/ppermute | solution.py:13
  113.0 84.4 %collective-permute-start.36 = (bf16[384,2048]{1,0:T(8,128)(2,1)S(1)}, bf16[384,2048]{1,0:T(8,128)(2,1)S(1)}, u32[]{:S(2)}, u32[]{:S(2)}) collective-permute-start(bf16[384,2048]{1,0:T(8,128)(2,1)S(1)} %add_convert_fusion), channel_id=1, source_target_pairs={{0,8},{8,0},{16,24},{24,16},{1,9},{9,1},{17,25},{25,17},{2,10},{10... | collective-permute-start | bytes 4718600 | tf_op jit(solution)/shard_map/ppermute | solution.py:13
  144.9 49.3 %collective-permute-start.26 = (bf16[192,2048]{1,0:T(8,128)(2,1)S(1)}, bf16[192,2048]{1,0:T(8,128)(2,1)S(1)}, u32[]{:S(2)}, u32[]{:S(2)}) collective-permute-start(bf16[192,2048]{1,0:T(8,128)(2,1)S(1)} %convolution_convert_fusion.6), channel_id=1, source_target_pairs={{0,16},{8,24},{16,0},{24,8},{1,17},{9,25},{17,1},{25,9},{2,18},{10... | collective-permute-start | bytes 2359304 | tf_op jit(solution)/shard_map/ppermute | solution.py:13
  146.0 60.2 %collective-permute-start = (s32[1,4]{1,0:T(1,128)}, s32[1,4]{1,0:T(1,128)}, u32[]{:S(2)}, u32[]{:S(2)}) collective-permute-start(s32[1,4]{1,0:T(1,128)} %param.8), channel_id=1, source_target_pairs={{0,8},{8,0},{16,24},{24,16},{1,9},{9,1},{17,25},{25,17},{2,10},{10... | collective-permute-start | bytes 56 | tf_op jit(solution)/shard_map/ppermute | solution.py:13
  149.4 102.8 %collective-permute-start.24 = (bf16[192,2048]{1,0:T(8,128)(2,1)}, bf16[192,2048]{1,0:T(8,128)(2,1)S(1)}, u32[]{:S(2)}, u32[]{:S(2)}) collective-permute-start(bf16[192,2048]{1,0:T(8,128)(2,1)} %convolution_convert_fusion.7), channel_id=1, source_target_pairs={{0,8},{8,0},{16,24},{24,16},{1,9},{9,1},{17,25},{25,17},{2,10},{10... | collective-permute-start | bytes 2359304 | tf_op jit(solution)/shard_map/ppermute | solution.py:13
  196.6 60.2 %collective-permute-start.27 = (bf16[192,2048]{1,0:T(8,128)(2,1)}, bf16[192,2048]{1,0:T(8,128)(2,1)}, u32[]{:S(2)}, u32[]{:S(2)}) collective-permute-start(bf16[192,2048]{1,0:T(8,128)(2,1)} %add_convert_fusion.7), channel_id=1, source_target_pairs={{0,8},{8,0},{16,24},{24,16},{1,9},{9,1},{17,25},{25,17},{2,10},{10... | collective-permute-start | bytes 2359304 | tf_op jit(solution)/shard_map/ppermute | solution.py:13
  202.1 84.2 %collective-permute-start.37 = (bf16[384,2048]{1,0:T(8,128)(2,1)}, bf16[384,2048]{1,0:T(8,128)(2,1)}, u32[]{:S(2)}, u32[]{:S(2)}) collective-permute-start(bf16[384,2048]{1,0:T(8,128)(2,1)} %get-tuple-element.113), channel_id=1, source_target_pairs={{0,8},{8,0},{16,24},{24,16},{1,9},{9,1},{17,25},{25,17},{2,10},{10... | collective-permute-start | bytes 4718600 | tf_op jit(solution)/shard_map/ppermute | solution.py:13
  203.3 83.0 %collective-permute-start.38 = (bf16[384,2048]{1,0:T(8,128)(2,1)}, bf16[384,2048]{1,0:T(8,128)(2,1)}, u32[]{:S(2)}, u32[]{:S(2)}) collective-permute-start(bf16[384,2048]{1,0:T(8,128)(2,1)} %get-tuple-element.113), channel_id=1, source_target_pairs={{0,16},{8,24},{16,0},{24,8},{1,17},{9,25},{17,1},{25,9},{2,18},{10... | collective-permute-start | bytes 4718600 | tf_op jit(solution)/shard_map/ppermute | solution.py:13
  206.1 32.4 %collective-permute-start.1 = (s32[1,4]{1,0:T(1,128)}, s32[1,4]{1,0:T(1,128)S(1)}, u32[]{:S(2)}, u32[]{:S(2)}) collective-permute-start(s32[1,4]{1,0:T(1,128)} %param.8), channel_id=1, source_target_pairs={{0,16},{8,24},{16,0},{24,8},{1,17},{9,25},{17,1},{25,9},{2,18},{10... | collective-permute-start | bytes 56 | tf_op jit(solution)/shard_map/ppermute | solution.py:13
  238.5 11.8 %collective-permute-start.2 = (s32[1,4]{1,0:T(1,128)}, s32[1,4]{1,0:T(1,128)S(1)}, u32[]{:S(2)}, u32[]{:S(2)}) collective-permute-start(s32[1,4]{1,0:T(1,128)} %param.8), channel_id=1, source_target_pairs={{0,24},{8,16},{16,8},{24,0},{1,25},{9,17},{17,9},{25,1},{2,26},{10... | collective-permute-start | bytes 56 | tf_op jit(solution)/shard_map/ppermute | solution.py:13
  251.5 39.3 %collective-permute-start.41 = (bf16[192,2048]{1,0:T(8,128)(2,1)}, bf16[192,2048]{1,0:T(8,128)(2,1)}, u32[]{:S(2)}, u32[]{:S(2)}) collective-permute-start(bf16[192,2048]{1,0:T(8,128)(2,1)} %convolution_convert_fusion.5), channel_id=1, source_target_pairs={{0,8},{8,0},{16,24},{24,16},{1,9},{9,1},{17,25},{25,17},{2,10},{10... | collective-permute-start | bytes 2359304 | tf_op jit(solution)/shard_map/ppermute | solution.py:13
  252.2 38.6 %collective-permute-start.42 = (bf16[192,2048]{1,0:T(8,128)(2,1)S(1)}, bf16[192,2048]{1,0:T(8,128)(2,1)}, u32[]{:S(2)}, u32[]{:S(2)}) collective-permute-start(bf16[192,2048]{1,0:T(8,128)(2,1)S(1)} %convolution_convert_fusion.4), channel_id=1, source_target_pairs={{0,16},{8,24},{16,0},{24,8},{1,17},{9,25},{17,1},{25,9},{2,18},{10... | collective-permute-start | bytes 2359304 | tf_op jit(solution)/shard_map/ppermute | solution.py:13
  256.8 29.5 %collective-permute-start.25 = (bf16[192,2048]{1,0:T(8,128)(2,1)}, bf16[192,2048]{1,0:T(8,128)(2,1)}, u32[]{:S(2)}, u32[]{:S(2)}) collective-permute-start(bf16[192,2048]{1,0:T(8,128)(2,1)} %add_convert_fusion.8), channel_id=1, source_target_pairs={{0,16},{8,24},{16,0},{24,8},{1,17},{9,25},{17,1},{25,9},{2,18},{10... | collective-permute-start | bytes 2359304 | tf_op jit(solution)/shard_map/ppermute | solution.py:13
  287.5 18.5 %collective-permute-start.39 = (bf16[192,2048]{1,0:T(8,128)(2,1)S(1)}, bf16[192,2048]{1,0:T(8,128)(2,1)S(1)}, u32[]{:S(2)}, u32[]{:S(2)}) collective-permute-start(bf16[192,2048]{1,0:T(8,128)(2,1)S(1)} %slice.176), channel_id=1, source_target_pairs={{0,8},{8,0},{16,24},{24,16},{1,9},{9,1},{17,25},{25,17},{2,10},{10... | collective-permute-start | bytes 2359304 | tf_op jit(solution)/shard_map/ppermute | solution.py:13
  290.4 20.5 %collective-permute-start.40 = (bf16[192,2048]{1,0:T(8,128)(2,1)S(1)}, bf16[192,2048]{1,0:T(8,128)(2,1)S(1)}, u32[]{:S(2)}, u32[]{:S(2)}) collective-permute-start(bf16[192,2048]{1,0:T(8,128)(2,1)S(1)} %slice.177), channel_id=1, source_target_pairs={{0,16},{8,24},{16,0},{24,8},{1,17},{9,25},{17,1},{25,9},{2,18},{10... | collective-permute-start | bytes 2359304 | tf_op jit(solution)/shard_map/ppermute | solution.py:13
  301.9 42.9 %collective-permute-start.48 = (bf16[384,2048]{1,0:T(8,128)(2,1)}, bf16[384,2048]{1,0:T(8,128)(2,1)}, u32[]{:S(2)}, u32[]{:S(2)}) collective-permute-start(bf16[384,2048]{1,0:T(8,128)(2,1)} %get-tuple-element.43), channel_id=1, source_target_pairs={{0,16},{8,24},{16,0},{24,8},{1,17},{9,25},{17,1},{25,9},{2,18},{10... | collective-permute-start | bytes 4718600 | tf_op jit(solution)/shard_map/ppermute | solution.py:13
  303.7 48.4 %collective-permute-start.47 = (bf16[384,2048]{1,0:T(8,128)(2,1)}, bf16[384,2048]{1,0:T(8,128)(2,1)}, u32[]{:S(2)}, u32[]{:S(2)}) collective-permute-start(bf16[384,2048]{1,0:T(8,128)(2,1)} %get-tuple-element.43), channel_id=1, source_target_pairs={{0,8},{8,0},{16,24},{24,16},{1,9},{9,1},{17,25},{25,17},{2,10},{10... | collective-permute-start | bytes 4718600 | tf_op jit(solution)/shard_map/ppermute | solution.py:13
  319.6 55.8 %collective-permute-start.50 = (bf16[384,2048]{1,0:T(8,128)(2,1)}, bf16[384,2048]{1,0:T(8,128)(2,1)}, u32[]{:S(2)}, u32[]{:S(2)}) collective-permute-start(bf16[384,2048]{1,0:T(8,128)(2,1)} %copy-done.35), channel_id=1, source_target_pairs={{0,16},{8,24},{16,0},{24,8},{1,17},{9,25},{17,1},{25,9},{2,18},{10... | collective-permute-start | bytes 4718600 | tf_op jit(solution)/shard_map/ppermute | solution.py:13
  322.7 58.7 %collective-permute-start.49 = (bf16[384,2048]{1,0:T(8,128)(2,1)}, bf16[384,2048]{1,0:T(8,128)(2,1)S(1)}, u32[]{:S(2)}, u32[]{:S(2)}) collective-permute-start(bf16[384,2048]{1,0:T(8,128)(2,1)} %copy-done.35), channel_id=1, source_target_pairs={{0,8},{8,0},{16,24},{24,16},{1,9},{9,1},{17,25},{25,17},{2,10},{10... | collective-permute-start | bytes 4718600 | tf_op jit(solution)/shard_map/ppermute | solution.py:13
  325.0 60.0 %collective-permute-start.44 = (bf16[1,384,128]{2,1,0:T(8,128)(2,1)S(1)}, bf16[1,384,128]{2,1,0:T(8,128)(2,1)S(1)}, u32[]{:S(2)}, u32[]{:S(2)}) collective-permute-start(bf16[1,384,128]{2,1,0:T(8,128)(2,1)S(1)} %get-tuple-element.79), channel_id=1, source_target_pairs={{0,2},{1,3},{2,4},{3,5},{4,6},{5,7},{6,0},{7,1},{8,10},{9,11},{10,... | collective-permute-start | bytes 294920 | tf_op jit(solution)/shard_map/ppermute | solution.py:30
  344.7 42.2 %collective-permute-start.46 = (bf16[1,384,128]{2,1,0:T(8,128)(2,1)S(1)}, bf16[1,384,128]{2,1,0:T(8,128)(2,1)S(1)}, u32[]{:S(2)}, u32[]{:S(2)}) collective-permute-start(bf16[1,384,128]{2,1,0:T(8,128)(2,1)S(1)} %get-tuple-element.77), channel_id=1, source_target_pairs={{0,6},{1,7},{2,0},{3,1},{4,2},{5,3},{6,4},{7,5},{8,14},{9,15},{10,... | collective-permute-start | bytes 294920 | tf_op jit(solution)/shard_map/ppermute | solution.py:30
  352.1 50.1 %collective-permute-start.55 = (bf16[192,2048]{1,0:T(8,128)(2,1)}, bf16[192,2048]{1,0:T(8,128)(2,1)}, u32[]{:S(2)}, u32[]{:S(2)}) collective-permute-start(bf16[192,2048]{1,0:T(8,128)(2,1)} %slice.238), channel_id=1, source_target_pairs={{0,8},{8,0},{16,24},{24,16},{1,9},{9,1},{17,25},{25,17},{2,10},{10... | collective-permute-start | bytes 2359304 | tf_op jit(solution)/shard_map/ppermute | solution.py:13
  375.4 35.4 %collective-permute-start.56 = (bf16[192,2048]{1,0:T(8,128)(2,1)}, bf16[192,2048]{1,0:T(8,128)(2,1)}, u32[]{:S(2)}, u32[]{:S(2)}) collective-permute-start(bf16[192,2048]{1,0:T(8,128)(2,1)} %slice.239), channel_id=1, source_target_pairs={{0,16},{8,24},{16,0},{24,8},{1,17},{9,25},{17,1},{25,9},{2,18},{10... | collective-permute-start | bytes 2359304 | tf_op jit(solution)/shard_map/ppermute | solution.py:13
  381.4 30.9 %collective-permute-start.57 = (bf16[192,2048]{1,0:T(8,128)(2,1)}, bf16[192,2048]{1,0:T(8,128)(2,1)}, u32[]{:S(2)}, u32[]{:S(2)}) collective-permute-start(bf16[192,2048]{1,0:T(8,128)(2,1)} %slice.240), channel_id=1, source_target_pairs={{0,8},{8,0},{16,24},{24,16},{1,9},{9,1},{17,25},{25,17},{2,10},{10... | collective-permute-start | bytes 2359304 | tf_op jit(solution)/shard_map/ppermute | solution.py:13
  385.1 27.3 %collective-permute-start.58 = (bf16[192,2048]{1,0:T(8,128)(2,1)}, bf16[192,2048]{1,0:T(8,128)(2,1)}, u32[]{:S(2)}, u32[]{:S(2)}) collective-permute-start(bf16[192,2048]{1,0:T(8,128)(2,1)} %slice.241), channel_id=1, source_target_pairs={{0,16},{8,24},{16,0},{24,8},{1,17},{9,25},{17,1},{25,9},{2,18},{10... | collective-permute-start | bytes 2359304 | tf_op jit(solution)/shard_map/ppermute | solution.py:13
  387.5 26.9 %collective-permute-start.51 = (bf16[2,384,512]{2,1,0:T(8,128)(2,1)S(1)}, bf16[2,384,512]{2,1,0:T(8,128)(2,1)}, u32[]{:S(2)}, u32[]{:S(2)}) collective-permute-start(bf16[2,384,512]{2,1,0:T(8,128)(2,1)S(1)} %fusion.51), channel_id=1, source_target_pairs={{0,1},{1,0},{2,3},{3,2},{4,5},{5,4},{6,7},{7,6},{8,9},{9,8},{10,11... | collective-permute-start | bytes 2359304 | tf_op jit(solution)/shard_map/ppermute | solution.py:35
  402.3 24.9 %collective-permute-start.45 = (bf16[1,384,128]{2,1,0:T(8,128)(2,1)}, bf16[1,384,128]{2,1,0:T(8,128)(2,1)S(1)}, u32[]{:S(2)}, u32[]{:S(2)}) collective-permute-start(bf16[1,384,128]{2,1,0:T(8,128)(2,1)} %get-tuple-element.78), channel_id=1, source_target_pairs={{0,4},{1,5},{2,6},{3,7},{4,0},{5,1},{6,2},{7,3},{8,12},{9,13},{10,... | collective-permute-start | bytes 294920 | tf_op jit(solution)/shard_map/ppermute | solution.py:30
  416.2 18.1 %collective-permute-start.53 = (bf16[2,384,128]{2,1,0:T(8,128)(2,1)S(1)}, bf16[2,384,128]{2,1,0:T(8,128)(2,1)S(1)}, u32[]{:S(2)}, u32[]{:S(2)}) collective-permute-start(bf16[2,384,128]{2,1,0:T(8,128)(2,1)S(1)} %get-tuple-element.69), channel_id=1, source_target_pairs={{0,4},{1,5},{2,6},{3,7},{4,0},{5,1},{6,2},{7,3},{8,12},{9,13},{10,... | collective-permute-start | bytes 589832 | tf_op jit(solution)/shard_map/ppermute | solution.py:30
  418.4 14.1 %collective-permute-start.52 = (bf16[2,384,128]{2,1,0:T(8,128)(2,1)S(1)}, bf16[2,384,128]{2,1,0:T(8,128)(2,1)S(1)}, u32[]{:S(2)}, u32[]{:S(2)}) collective-permute-start(bf16[2,384,128]{2,1,0:T(8,128)(2,1)S(1)} %get-tuple-element.70), channel_id=1, source_target_pairs={{0,2},{1,3},{2,4},{3,5},{4,6},{5,7},{6,0},{7,1},{8,10},{9,11},{10,... | collective-permute-start | bytes 589832 | tf_op jit(solution)/shard_map/ppermute | solution.py:30
  421.4 12.8 %collective-permute-start.54 = (bf16[2,384,128]{2,1,0:T(8,128)(2,1)S(1)}, bf16[2,384,128]{2,1,0:T(8,128)(2,1)S(1)}, u32[]{:S(2)}, u32[]{:S(2)}) collective-permute-start(bf16[2,384,128]{2,1,0:T(8,128)(2,1)S(1)} %get-tuple-element.68), channel_id=1, source_target_pairs={{0,6},{1,7},{2,0},{3,1},{4,2},{5,3},{6,4},{7,5},{8,14},{9,15},{10,... | collective-permute-start | bytes 589832 | tf_op jit(solution)/shard_map/ppermute | solution.py:30
  427.0 7.2 %collective-permute-start.59 = (bf16[1,384,512]{2,1,0:T(8,128)(2,1)S(1)}, bf16[1,384,512]{2,1,0:T(8,128)(2,1)S(1)}, u32[]{:S(2)}, u32[]{:S(2)}) collective-permute-start(bf16[1,384,512]{2,1,0:T(8,128)(2,1)S(1)} %dynamic-slice_bitcast_fusion), channel_id=1, source_target_pairs={{0,1},{1,0},{2,3},{3,2},{4,5},{5,4},{6,7},{7,6},{8,9},{9,8},{10,11... | collective-permute-start | bytes 1179656 | tf_op jit(solution)/shard_map/ppermute | solution.py:35
  434.5 11.5 %collective-permute-start.61 = (bf16[1,384,128]{2,1,0:T(8,128)(2,1)S(1)}, bf16[1,384,128]{2,1,0:T(8,128)(2,1)S(1)}, u32[]{:S(2)}, u32[]{:S(2)}) collective-permute-start(bf16[1,384,128]{2,1,0:T(8,128)(2,1)S(1)} %get-tuple-element.82), channel_id=1, source_target_pairs={{0,4},{1,5},{2,6},{3,7},{4,0},{5,1},{6,2},{7,3},{8,12},{9,13},{10,... | collective-permute-start | bytes 294920 | tf_op jit(solution)/shard_map/ppermute | solution.py:30
  438.1 7.5 %collective-permute-start.60 = (bf16[1,384,128]{2,1,0:T(8,128)(2,1)S(1)}, bf16[1,384,128]{2,1,0:T(8,128)(2,1)S(1)}, u32[]{:S(2)}, u32[]{:S(2)}) collective-permute-start(bf16[1,384,128]{2,1,0:T(8,128)(2,1)S(1)} %get-tuple-element.83), channel_id=1, source_target_pairs={{0,2},{1,3},{2,4},{3,5},{4,6},{5,7},{6,0},{7,1},{8,10},{9,11},{10,... | collective-permute-start | bytes 294920 | tf_op jit(solution)/shard_map/ppermute | solution.py:30
  438.1 7.5 %collective-permute-start.62 = (bf16[1,384,128]{2,1,0:T(8,128)(2,1)S(1)}, bf16[1,384,128]{2,1,0:T(8,128)(2,1)S(1)}, u32[]{:S(2)}, u32[]{:S(2)}) collective-permute-start(bf16[1,384,128]{2,1,0:T(8,128)(2,1)S(1)} %get-tuple-element.81), channel_id=1, source_target_pairs={{0,6},{1,7},{2,0},{3,1},{4,2},{5,3},{6,4},{7,5},{8,14},{9,15},{10,... | collective-permute-start | bytes 294920 | tf_op jit(solution)/shard_map/ppermute | solution.py:30
  448.8 16.1 %all-to-all-start = ((bf16[4,576,128]{2,1,0:T(8,128)(2,1)}), bf16[4,576,128]{2,1,0:T(8,128)(2,1)S(1)}, u32[]{:S(2)}, u32[]{:S(2)}) async-start(bf16[4,576,128]{2,1,0:T(8,128)(2,1)} %fusion.61), calls=%async_computation | async-start | bytes 1179648 | tf_op jit(solution)/shard_map/all_to_all | solution.py:143
  465.0 16.2 %collective-permute-start.63 = (bf16[576,128]{1,0:T(8,128)(2,1)S(1)}, bf16[576,128]{1,0:T(8,128)(2,1)S(1)}, u32[]{:S(2)}, u32[]{:S(2)}) collective-permute-start(bf16[576,128]{1,0:T(8,128)(2,1)S(1)} %get-tuple-element.76), channel_id=1, source_target_pairs={{0,6},{1,7},{2,0},{3,1},{4,2},{5,3},{6,4},{7,5},{8,14},{9,15},{10,... | collective-permute-start | bytes 442376 | tf_op jit(solution)/shard_map/ppermute | solution.py:30
  468.0 13.3 %collective-permute-start.64 = (bf16[576,128]{1,0:T(8,128)(2,1)S(1)}, bf16[576,128]{1,0:T(8,128)(2,1)S(1)}, u32[]{:S(2)}, u32[]{:S(2)}) collective-permute-start(bf16[576,128]{1,0:T(8,128)(2,1)S(1)} %get-tuple-element.75), channel_id=1, source_target_pairs={{0,4},{1,5},{2,6},{3,7},{4,0},{5,1},{6,2},{7,3},{8,12},{9,13},{10,... | collective-permute-start | bytes 442376 | tf_op jit(solution)/shard_map/ppermute | solution.py:30
  468.6 12.7 %collective-permute-start.65 = (bf16[576,128]{1,0:T(8,128)(2,1)S(1)}, bf16[576,128]{1,0:T(8,128)(2,1)S(1)}, u32[]{:S(2)}, u32[]{:S(2)}) collective-permute-start(bf16[576,128]{1,0:T(8,128)(2,1)S(1)} %get-tuple-element.74), channel_id=1, source_target_pairs={{0,2},{1,3},{2,4},{3,5},{4,6},{5,7},{6,0},{7,1},{8,10},{9,11},{10,... | collective-permute-start | bytes 442376 | tf_op jit(solution)/shard_map/ppermute | solution.py:30
  (45 other events, 948.9 us)
where the time goes:
time: 486 us; the launch traced here: 483 us
  waiting for transfers between devices  220 us (45%)
  starting transfers between devices  118 us (24%)
  matrix products  101 us (21%)
  local copies, waits for them, and re-layouts  23.5 us (5%)
  other arithmetic  17.8 us (4%)
    ppermute x33, waiting for transfers between devices, swap(): return lax.ppermute(values, 'fsdp', [(i, i ^ offset) for i in range(size)])  183 us
    ppermute x27, starting transfers between devices, shift_line(): return lax.ppermute(values, 'tensor', pairs)  78.6 us
    dot_general x15, matrix products, matmul_t(): lax.dot_general(left_side, right_side, (((1,), (1,)), ((), ())), preferre...  48.5 us
    ppermute x27, waiting for transfers between devices, shift_line(): return lax.ppermute(values, 'tensor', pairs)  36.3 us
    ppermute x33, starting transfers between devices, swap(): return lax.ppermute(values, 'fsdp', [(i, i ^ offset) for i in range(size)])  35.9 us
    dot_general x3, matrix products, contract_rows(): lax.dot_general(left_side, right_side, (((0,), (0,)), ((), ())), preferre...  35.5 us
    dot_general x8, matrix products, matmul(): return jnp.dot(left_side, right_side, preferred_element_type=jnp.float32)  17.2 us
  transfers between devices with their start and end apart: 67, of which 23 were waited for; matrix products, arithmetic and copies ran while one was open for 28% of the time, Pallas kernels for 0%

commit v1 on v0

--- a/solution.py
+++ b/solution.py
@@ -35,6 +35,16 @@
         return lax.ppermute(values, "tensor", pairs)
 
 
+def across(grid, values, target):
+    n, m, wide = grid.n, grid.m, grid.wide
+    pairs = []
+    for f in range(n):
+        for t in range(wide):
+            to_f, to_line = target(f, t // m)
+            pairs.append((f * wide + t, to_f * wide + to_line * m + t % m))
+    return lax.ppermute(values, ("fsdp", "tensor"), pairs)
+
+
 def matmul(left_side, right_side):
     return jnp.dot(left_side, right_side, preferred_element_type=jnp.float32)
 
@@ -59,21 +69,18 @@
     n = grid.n
     quarters = rows.reshape(n, rows.shape[0] // n, rows.shape[1])
     turns = []
-    for r in range(n):
-        quarter = lax.dynamic_index_in_dim(quarters, (grid.line + r) % n, axis=0, keepdims=False)
-        turns.append(grid.shift_line(quarter, r) if r else quarter)
+    for k in range(n):
+        quarter = lax.dynamic_index_in_dim(quarters, (grid.me + k) % n, axis=0, keepdims=False)
+        turns.append(across(grid, quarter, lambda f, line, k=k: (line, (f + k) % n)))
     return turns
 
 
-def to_learner_features(grid, turns):
+def by_shard(grid, turns):
     turns = jnp.stack(turns)
-    piece = {}
-    for k in range(grid.n):
-        turn = (grid.line - (grid.me ^ k)) % grid.n
-        piece[k] = lax.dynamic_index_in_dim(turns, turn, axis=0, keepdims=False)
-        if k:
-            piece[k] = swap(piece[k], k)
-    return piece
+    return [
+        lax.dynamic_index_in_dim(turns, (grid.line - (grid.me ^ k)) % grid.n, 0, keepdims=False)
+        for k in range(grid.n)
+    ]
 
 
 def all_places(grid, mine):
@@ -175,7 +182,7 @@
 
     turns = hand_out(grid, inputs_roll)
     *turns, cotangent_roll = fence(*turns, cotangent_roll)
-    piece = to_learner_features(grid, turns)
+    piece = by_shard(grid, turns)
     half3 = all_places(grid, piece[3][None])
     cot_turns = hand_out(grid, cotangent_roll)
     in3 = all_sides(grid, half3)[0]
@@ -183,7 +190,7 @@
 
     g3_came, u3_came = swap_x(g3), swap_y(u3)
     half_others = all_places(grid, jnp.stack([piece[1], piece[2], piece[0]]))
-    cot_piece = to_learner_features(grid, cot_turns)
+    cot_piece = by_shard(grid, cot_turns)
     in1, in2, in0 = all_sides(grid, half_others)
     g1, u2 = low(matmul(in1, w_gate)), low(matmul(in2, w_up))
 

time: 486 us -> 494 us (1.016)
  starting transfers between devices: 118 us -> 149 us
  waiting for transfers between devices: 220 us -> 198 us
    ppermute x33 -> x27, starting transfers between devices: 35.9 us -> 61.3 us  [swap(): return lax.ppermute(values, 'fsdp', [(i, i ^ offset) for i in range(size)])]
    ppermute x0 -> x8, starting transfers between devices: none -> 22.5 us  [across(): return lax.ppermute(values, ('fsdp', 'tensor'), pairs)]
    ppermute x27 -> x21, waiting for transfers between devices: 36.3 us -> 14.1 us  [shift_line(): return lax.ppermute(values, 'tensor', pairs)]
    ppermute x27 -> x21, starting transfers between devices: 78.6 us -> 61.7 us  [shift_line(): return lax.ppermute(values, 'tensor', pairs)]
    ppermute x33 -> x27, waiting for transfers between devices: 183 us -> 180 us  [swap(): return lax.ppermute(values, 'fsdp', [(i, i ^ offset) for i in range(size)])]
  transfers between devices with their start and end apart: 67 -> 63, of which waited for: 23 -> 23; matrix products, arithmetic and copies ran while one was open for 28% -> 27% of each run, Pallas kernels for 0% -> 0%
where the time goes in v1:
time: 494 us; the launch traced here: 490 us
  waiting for transfers between devices  198 us (40%)
  starting transfers between devices  149 us (30%)
  matrix products  101 us (20%)
  local copies, waits for them, and re-layouts  22.4 us (5%)
  other arithmetic  17.5 us (4%)
    ppermute x27, waiting for transfers between devices, swap(): return lax.ppermute(values, 'fsdp', [(i, i ^ offset) for i in range(size)])  180 us
    ppermute x21, starting transfers between devices, shift_line(): return lax.ppermute(values, 'tensor', pairs)  61.7 us
    ppermute x27, starting transfers between devices, swap(): return lax.ppermute(values, 'fsdp', [(i, i ^ offset) for i in range(size)])  61.3 us
    dot_general x15, matrix products, matmul_t(): lax.dot_general(left_side, right_side, (((1,), (1,)), ((), ())), preferre...  48.3 us
    dot_general x3, matrix products, contract_rows(): lax.dot_general(left_side, right_side, (((0,), (0,)), ((), ())), preferre...  35.5 us
    ppermute x8, starting transfers between devices, across(): return lax.ppermute(values, ('fsdp', 'tensor'), pairs)  22.5 us
    dot_general x8, matrix products, matmul(): return jnp.dot(left_side, right_side, preferred_element_type=jnp.float32)  17.2 us
    ppermute x21, waiting for transfers between devices, shift_line(): return lax.ppermute(values, 'tensor', pairs)  14.1 us
  transfers between devices with their start and end apart: 63, of which 23 were waited for; matrix products, arithmetic and copies ran while one was open for 27% of the time, Pallas kernels for 0%

profile of v1, /device:TPU:0, one launch (start us, length us, event | category | flops | bytes accessed | tf_op | source)
XLA Modules:
  0.0 490.2 jit_solution(4580995920793253064)
XLA Ops:
  2.5 5.7 %collective-permute-start.4 = (bf16[96,512]{1,0:T(8,128)(2,1)S(1)}, bf16[96,512]{1,0:T(8,128)(2,1)S(1)}, u32[]{:S(2)}, u32[]{:S(2)}) collective-permute-start(bf16[96,512]{1,0:T(8,128)(2,1)S(1)} %get-tuple-element.101), channel_id=1, source_target_pairs={{0,2},{1,3},{2,10},{3,11},{4,18},{5,19},{6,26},{7,27},{8,4},{9,5},... | collective-permute-start | bytes 294920 | tf_op jit(solution)/shard_map/ppermute | solution.py:45
  8.2 3.5 collective-permute-start.5
  11.7 2.3 collective-permute-start.6
  15.9 1.8 collective-permute-done.6
  17.8 1.9 collective-permute-start.25
  19.7 2.3 collective-permute-start.26
  22.0 2.8 collective-permute-start.27
  25.7 4.6 collective-permute-start.8
  30.3 2.3 collective-permute-start.9
  32.7 2.7 collective-permute-start.10
  35.4 7.7 %collective-permute-start.16 = (bf16[3,96,512]{2,1,0:T(8,128)(2,1)S(1)}, bf16[3,96,512]{2,1,0:T(8,128)(2,1)S(1)}, u32[]{:S(2)}, u32[]{:S(2)}) collective-permute-start(bf16[3,96,512]{2,1,0:T(8,128)(2,1)S(1)} %get-tuple-element.104), channel_id=1, source_target_pairs={{0,4},{1,5},{2,6},{3,7},{4,0},{5,1},{6,2},{7,3},{8,12},{9,13},{10,... | collective-permute-start | bytes 884744 | tf_op jit(solution)/shard_map/ppermute | solution.py:30
  43.2 2.0 collective-permute-start.17
  45.4 10.5 %collective-permute-start.11 = (bf16[4,96,512]{2,1,0:T(8,128)(2,1)S(1)}, bf16[4,96,512]{2,1,0:T(8,128)(2,1)S(1)}, u32[]{:S(2)}, u32[]{:S(2)}) collective-permute-start(bf16[4,96,512]{2,1,0:T(8,128)(2,1)S(1)} %get-tuple-element.90), channel_id=1, source_target_pairs={{0,2},{1,3},{2,4},{3,5},{4,6},{5,7},{6,0},{7,1},{8,10},{9,11},{10,... | collective-permute-start | bytes 1179656 | tf_op jit(solution)/shard_map/ppermute | solution.py:30
  57.7 9.2 %collective-permute-start.13 = (bf16[4,96,512]{2,1,0:T(8,128)(2,1)S(1)}, bf16[4,96,512]{2,1,0:T(8,128)(2,1)S(1)}, u32[]{:S(2)}, u32[]{:S(2)}) collective-permute-start(bf16[4,96,512]{2,1,0:T(8,128)(2,1)S(1)} %get-tuple-element.90), channel_id=1, source_target_pairs={{0,6},{1,7},{2,0},{3,1},{4,2},{5,3},{6,4},{7,5},{8,14},{9,15},{10,... | collective-permute-start | bytes 1179656 | tf_op jit(solution)/shard_map/ppermute | solution.py:30
  67.3 1.8 convolution_convert_fusion.1
  69.1 5.5 %collective-permute-start.29 = (bf16[384,2048]{1,0:T(8,128)(2,1)S(1)}, bf16[384,2048]{1,0:T(8,128)(2,1)S(1)}, u32[]{:S(2)}, u32[]{:S(2)}) collective-permute-start(bf16[384,2048]{1,0:T(8,128)(2,1)S(1)} %convolution_convert_fusion.1), channel_id=1, source_target_pairs={{0,8},{8,0},{16,24},{24,16},{1,9},{9,1},{17,25},{25,17},{2,10},{10... | collective-permute-start | bytes 4718600 | tf_op jit(solution)/shard_map/ppermute | solution.py:13
  74.6 1.8 convolution_convert_fusion
  76.4 11.3 %collective-permute-start.31 = (bf16[384,2048]{1,0:T(8,128)(2,1)S(1)}, bf16[384,2048]{1,0:T(8,128)(2,1)S(1)}, u32[]{:S(2)}, u32[]{:S(2)}) collective-permute-start(bf16[384,2048]{1,0:T(8,128)(2,1)S(1)} %convolution_convert_fusion), channel_id=1, source_target_pairs={{0,16},{8,24},{16,0},{24,8},{1,17},{9,25},{17,1},{25,9},{2,18},{10... | collective-permute-start | bytes 4718600 | tf_op jit(solution)/shard_map/ppermute | solution.py:13
  91.6 6.3 %collective-permute-start.20 = (bf16[384,2048]{1,0:T(8,128)(2,1)S(1)}, bf16[384,2048]{1,0:T(8,128)(2,1)S(1)}, u32[]{:S(2)}, u32[]{:S(2)}) collective-permute-start(bf16[384,2048]{1,0:T(8,128)(2,1)S(1)} %convolution_convert_fusion.2), channel_id=1, source_target_pairs={{0,16},{8,24},{16,0},{24,8},{1,17},{9,25},{17,1},{25,9},{2,18},{10... | collective-permute-start | bytes 4718600 | tf_op jit(solution)/shard_map/ppermute | solution.py:13
  99.8 10.0 %collective-permute-done.29 = bf16[384,2048]{1,0:T(8,128)(2,1)S(1)} collective-permute-done((bf16[384,2048]{1,0:T(8,128)(2,1)S(1)}, bf16[384,2048]{1,0:T(8,128)(2,1)S(1)}, u32[]{:S(2)}, u32[]{:S(2)}) %collective-permute-start.29) | collective-permute-done | bytes 1572896 | tf_op jit(solution)/shard_map/ppermute | solution.py:13
  111.6 11.3 %collective-permute-start.30 = (bf16[384,2048]{1,0:T(8,128)(2,1)S(1)}, bf16[384,2048]{1,0:T(8,128)(2,1)S(1)}, u32[]{:S(2)}, u32[]{:S(2)}) collective-permute-start(bf16[384,2048]{1,0:T(8,128)(2,1)S(1)} %add_convert_fusion.1), channel_id=1, source_target_pairs={{0,16},{8,24},{16,0},{24,8},{1,17},{9,25},{17,1},{25,9},{2,18},{10... | collective-permute-start | bytes 4718600 | tf_op jit(solution)/shard_map/ppermute | solution.py:13
  123.0 1.8 add_convert_fusion
  124.8 2.0 collective-permute-start.32
  129.5 2.5 convolution_convert_fusion.7
  132.0 1.9 convolution_convert_fusion.4
  133.9 2.4 convolution_convert_fusion.5
  136.3 20.3 %collective-permute-done.20 = bf16[384,2048]{1,0:T(8,128)(2,1)S(1)} collective-permute-done((bf16[384,2048]{1,0:T(8,128)(2,1)S(1)}, bf16[384,2048]{1,0:T(8,128)(2,1)S(1)}, u32[]{:S(2)}, u32[]{:S(2)}) %collective-permute-start.20) | collective-permute-done | bytes 1572896 | tf_op jit(solution)/shard_map/ppermute | solution.py:13
  156.7 2.1 collective-permute-start.23
  163.2 43.5 %collective-permute-done.23 = bf16[192,2048]{1,0:T(8,128)(2,1)S(1)} collective-permute-done((bf16[192,2048]{1,0:T(8,128)(2,1)S(1)}, bf16[192,2048]{1,0:T(8,128)(2,1)S(1)}, u32[]{:S(2)}, u32[]{:S(2)}) %collective-permute-start.23) | collective-permute-done | bytes 786464 | tf_op jit(solution)/shard_map/ppermute | solution.py:13
  206.7 2.4 add_convert_fusion.7
  210.1 4.6 multiply_convert_fusion.2
  219.2 32.3 %collective-permute-done.1 = s32[1,4]{1,0:T(1,128)S(1)} collective-permute-done((s32[1,4]{1,0:T(1,128)}, s32[1,4]{1,0:T(1,128)S(1)}, u32[]{:S(2)}, u32[]{:S(2)}) %collective-permute-start.1) | collective-permute-done | bytes 48 | tf_op jit(solution)/shard_map/ppermute | solution.py:13
  251.5 2.0 collective-permute-start.2
  253.5 9.6 %collective-permute-done.2 = s32[1,4]{1,0:T(1,128)S(1)} collective-permute-done((s32[1,4]{1,0:T(1,128)}, s32[1,4]{1,0:T(1,128)S(1)}, u32[]{:S(2)}, u32[]{:S(2)}) %collective-permute-start.2) | collective-permute-done | bytes 48 | tf_op jit(solution)/shard_map/ppermute | solution.py:13
  266.0 4.6 add_convert_fusion.8
  273.9 26.1 %collective-permute-done.22 = bf16[192,2048]{1,0:T(8,128)(2,1)} collective-permute-done((bf16[192,2048]{1,0:T(8,128)(2,1)}, bf16[192,2048]{1,0:T(8,128)(2,1)}, u32[]{:S(2)}, u32[]{:S(2)}) %collective-permute-start.22) | collective-permute-done | bytes 786464 | tf_op jit(solution)/shard_map/ppermute | solution.py:13
  304.1 11.0 %multiply_convert_fusion = (bf16[384,2048]{1,0:T(8,128)(2,1)}, bf16[384,2048]{1,0:T(8,128)(2,1)S(1)}) fusion(bf16[384,2048]{1,0:T(8,128)(2,1)} %copy-done.39, f32[384,2048]{1,0:T(8,128)} %copy-done.42, bf16[384,2048]{1,0:T(8,128)(2,1)} %copy-done.38, bf16[384,2048]{1,0:T(8,128)(2,1)} %copy-done.40, f32[384,2048]{1,0:T(8,128)} %get-tuple-element.114, ...), kind=kOutput, calls=%fused_computation.45 | convolution fusion | flops 1636564992 | bytes 23855104 | tf_op jit(solution)/shard_map/dot_general | solution.py:53
  317.8 3.0 collective-permute-done.35
  320.8 2.9 collective-permute-done.36
  323.8 1.8 fusion.134
  326.0 3.4 add_convert_fusion.6
  339.5 4.8 collective-permute-start.40
  344.3 13.1 %collective-permute-done.44 = bf16[384,2048]{1,0:T(8,128)(2,1)} collective-permute-done((bf16[384,2048]{1,0:T(8,128)(2,1)}, bf16[384,2048]{1,0:T(8,128)(2,1)}, u32[]{:S(2)}, u32[]{:S(2)}) %collective-permute-start.44) | collective-permute-done | bytes 1572896 | tf_op jit(solution)/shard_map/ppermute | solution.py:13
  357.7 4.6 fusion.136
  362.3 2.1 slice.238
  365.8 3.4 fusion.135
  369.2 2.1 slice.239
  371.3 16.9 %collective-permute-done.46 = bf16[384,2048]{1,0:T(8,128)(2,1)} collective-permute-done((bf16[384,2048]{1,0:T(8,128)(2,1)}, bf16[384,2048]{1,0:T(8,128)(2,1)}, u32[]{:S(2)}, u32[]{:S(2)}) %collective-permute-start.46) | collective-permute-done | bytes 1572896 | tf_op jit(solution)/shard_map/ppermute | solution.py:13
  389.0 2.1 slice.240
  391.1 3.2 fusion.138
  396.1 1.8 fusion.137
  401.3 11.4 %fusion.24 = bf16[2048,1024]{1,0:T(8,128)(2,1)} fusion(bf16[384,2048]{1,0:T(8,128)(2,1)S(1)} %pad_maximum_fusion.1, bf16[384,2048]{1,0:T(8,128)(2,1)} %collective-permute-done.34, bf16[384,2048]{1,0:T(8,128)(2,1)} %collective-permute-done.33, bf16[384,2048]{1,0:T(8,128)(2,1)} %get-tuple-element.113, bf16[384,512]{1,0:T(8,128)(2,1)S(1)} %bitcast.174, ...), kind=kOutput, calls=%fused_computation.26 | convolution fusion | flops 6494879744 | bytes 13631488 | tf_op jit(solution)/shard_map/dot_general | solution.py:59
  425.1 4.0 collective-permute-start.48
  430.8 1.8 fusion.139
  432.7 1.9 add_convert_fusion.2
  434.7 5.5 %collective-permute-done.48 = bf16[2,384,128]{2,1,0:T(8,128)(2,1)S(1)} collective-permute-done((bf16[2,384,128]{2,1,0:T(8,128)(2,1)S(1)}, bf16[2,384,128]{2,1,0:T(8,128)(2,1)S(1)}, u32[]{:S(2)}, u32[]{:S(2)}) %collective-permute-start.48) | collective-permute-done | bytes 196640 | tf_op jit(solution)/shard_map/ppermute | solution.py:30
  441.1 4.2 collective-permute-start.57
  445.4 3.8 collective-permute-start.58
  449.3 3.4 collective-permute-done.56
  454.5 2.0 fusion.61
  456.5 3.7 all-to-all-start
  460.3 12.3 %fusion.27 = bf16[1024,2048]{1,0:T(8,128)(2,1)} fusion(bf16[384,2048]{1,0:T(8,128)(2,1)} %copy-done.1, bf16[384,2048]{1,0:T(8,128)(2,1)} %collective-permute-done.44, bf16[384,2048]{1,0:T(8,128)(2,1)} %collective-permute-done.43, bf16[384,2048]{1,0:T(8,128)(2,1)} %get-tuple-element.43, bf16[384,512]{1,0:T(8,128)(2,1)} %bitcast.222, ...), kind=kOutput, calls=%fused_computation.27 | convolution fusion | flops 6494879744 | bytes 13631488 | tf_op jit(solution)/shard_map/dot_general | solution.py:59
  472.6 2.6 collective-permute-start.59
  476.8 11.7 %fusion.30 = bf16[1024,2048]{1,0:T(8,128)(2,1)} fusion(bf16[384,2048]{1,0:T(8,128)(2,1)S(1)} %pad_maximum_fusion.3, bf16[384,2048]{1,0:T(8,128)(2,1)} %collective-permute-done.46, bf16[384,2048]{1,0:T(8,128)(2,1)} %copy-done.14, bf16[384,2048]{1,0:T(8,128)(2,1)} %copy-done.41, bf16[384,512]{1,0:T(8,128)(2,1)} %bitcast.223, bf16[384,512]{1,0:T(8,128)(2,1)} %bitcast.219, ...), kind=kOutput, calls=%fused_computation.28 | convolution fusion | flops 6494879744 | bytes 13631488 | tf_op jit(solution)/shard_map/dot_general | solution.py:59
  (255 shorter events, 77.7 us)
Async XLA Ops:
  1.8 12.2 %collective-permute-start.3 = (bf16[96,512]{1,0:T(8,128)(2,1)S(1)}, bf16[96,512]{1,0:T(8,128)(2,1)S(1)}, u32[]{:S(2)}, u32[]{:S(2)}) collective-permute-start(bf16[96,512]{1,0:T(8,128)(2,1)S(1)} %get-tuple-element.102), channel_id=1, source_target_pairs={{0,0},{1,1},{2,8},{3,9},{4,16},{5,17},{6,24},{7,25},{8,2},{9,3},{1... | collective-permute-start | bytes 294920 | tf_op jit(solution)/shard_map/ppermute | solution.py:45
  2.5 12.9 %collective-permute-start.4 = (bf16[96,512]{1,0:T(8,128)(2,1)S(1)}, bf16[96,512]{1,0:T(8,128)(2,1)S(1)}, u32[]{:S(2)}, u32[]{:S(2)}) collective-permute-start(bf16[96,512]{1,0:T(8,128)(2,1)S(1)} %get-tuple-element.101), channel_id=1, source_target_pairs={{0,2},{1,3},{2,10},{3,11},{4,18},{5,19},{6,26},{7,27},{8,4},{9,5},... | collective-permute-start | bytes 294920 | tf_op jit(solution)/shard_map/ppermute | solution.py:45
  8.2 7.7 %collective-permute-start.5 = (bf16[96,512]{1,0:T(8,128)(2,1)S(1)}, bf16[96,512]{1,0:T(8,128)(2,1)S(1)}, u32[]{:S(2)}, u32[]{:S(2)}) collective-permute-start(bf16[96,512]{1,0:T(8,128)(2,1)S(1)} %get-tuple-element.100), channel_id=1, source_target_pairs={{0,4},{1,5},{2,12},{3,13},{4,20},{5,21},{6,28},{7,29},{8,6},{9,7},... | collective-permute-start | bytes 294920 | tf_op jit(solution)/shard_map/ppermute | solution.py:45
  11.7 6.0 %collective-permute-start.6 = (bf16[96,512]{1,0:T(8,128)(2,1)S(1)}, bf16[96,512]{1,0:T(8,128)(2,1)S(1)}, u32[]{:S(2)}, u32[]{:S(2)}) collective-permute-start(bf16[96,512]{1,0:T(8,128)(2,1)S(1)} %get-tuple-element.99), channel_id=1, source_target_pairs={{0,6},{1,7},{2,14},{3,15},{4,22},{5,23},{6,30},{7,31},{8,0},{9,1},... | collective-permute-start | bytes 294920 | tf_op jit(solution)/shard_map/ppermute | solution.py:45
  17.8 7.9 %collective-permute-start.25 = (bf16[1,96,512]{2,1,0:T(8,128)(2,1)S(1)}, bf16[1,96,512]{2,1,0:T(8,128)(2,1)S(1)}, u32[]{:S(2)}, u32[]{:S(2)}) collective-permute-start(bf16[1,96,512]{2,1,0:T(8,128)(2,1)S(1)} %get-tuple-element.85), channel_id=1, source_target_pairs={{0,2},{1,3},{2,4},{3,5},{4,6},{5,7},{6,0},{7,1},{8,10},{9,11},{10,... | collective-permute-start | bytes 294920 | tf_op jit(solution)/shard_map/ppermute | solution.py:30
  19.7 10.7 %collective-permute-start.26 = (bf16[1,96,512]{2,1,0:T(8,128)(2,1)S(1)}, bf16[1,96,512]{2,1,0:T(8,128)(2,1)S(1)}, u32[]{:S(2)}, u32[]{:S(2)}) collective-permute-start(bf16[1,96,512]{2,1,0:T(8,128)(2,1)S(1)} %get-tuple-element.85), channel_id=1, source_target_pairs={{0,4},{1,5},{2,6},{3,7},{4,0},{5,1},{6,2},{7,3},{8,12},{9,13},{10,... | collective-permute-start | bytes 294920 | tf_op jit(solution)/shard_map/ppermute | solution.py:30
  22.0 10.7 %collective-permute-start.27 = (bf16[1,96,512]{2,1,0:T(8,128)(2,1)S(1)}, bf16[1,96,512]{2,1,0:T(8,128)(2,1)S(1)}, u32[]{:S(2)}, u32[]{:S(2)}) collective-permute-start(bf16[1,96,512]{2,1,0:T(8,128)(2,1)S(1)} %get-tuple-element.85), channel_id=1, source_target_pairs={{0,6},{1,7},{2,0},{3,1},{4,2},{5,3},{6,4},{7,5},{8,14},{9,15},{10,... | collective-permute-start | bytes 294920 | tf_op jit(solution)/shard_map/ppermute | solution.py:30
  24.9 31.0 %collective-permute-start.15 = (bf16[3,96,512]{2,1,0:T(8,128)(2,1)S(1)}, bf16[3,96,512]{2,1,0:T(8,128)(2,1)S(1)}, u32[]{:S(2)}, u32[]{:S(2)}) collective-permute-start(bf16[3,96,512]{2,1,0:T(8,128)(2,1)S(1)} %get-tuple-element.104), channel_id=1, source_target_pairs={{0,2},{1,3},{2,4},{3,5},{4,6},{5,7},{6,0},{7,1},{8,10},{9,11},{10,... | collective-permute-start | bytes 884744 | tf_op jit(solution)/shard_map/ppermute | solution.py:30
  25.0 10.4 %collective-permute-start.7 = (bf16[96,512]{1,0:T(8,128)(2,1)S(1)}, bf16[96,512]{1,0:T(8,128)(2,1)S(1)}, u32[]{:S(2)}, u32[]{:S(2)}) collective-permute-start(bf16[96,512]{1,0:T(8,128)(2,1)S(1)} %get-tuple-element.95), channel_id=1, source_target_pairs={{0,0},{1,1},{2,8},{3,9},{4,16},{5,17},{6,24},{7,25},{8,2},{9,3},{1... | collective-permute-start | bytes 294920 | tf_op jit(solution)/shard_map/ppermute | solution.py:45
  25.7 17.5 %collective-permute-start.8 = (bf16[96,512]{1,0:T(8,128)(2,1)S(1)}, bf16[96,512]{1,0:T(8,128)(2,1)S(1)}, u32[]{:S(2)}, u32[]{:S(2)}) collective-permute-start(bf16[96,512]{1,0:T(8,128)(2,1)S(1)} %get-tuple-element.98), channel_id=1, source_target_pairs={{0,2},{1,3},{2,10},{3,11},{4,18},{5,19},{6,26},{7,27},{8,4},{9,5},... | collective-permute-start | bytes 294920 | tf_op jit(solution)/shard_map/ppermute | solution.py:45
  30.3 14.9 %collective-permute-start.9 = (bf16[96,512]{1,0:T(8,128)(2,1)S(1)}, bf16[96,512]{1,0:T(8,128)(2,1)S(1)}, u32[]{:S(2)}, u32[]{:S(2)}) collective-permute-start(bf16[96,512]{1,0:T(8,128)(2,1)S(1)} %get-tuple-element.97), channel_id=1, source_target_pairs={{0,4},{1,5},{2,12},{3,13},{4,20},{5,21},{6,28},{7,29},{8,6},{9,7},... | collective-permute-start | bytes 294920 | tf_op jit(solution)/shard_map/ppermute | solution.py:45
  32.7 12.5 %collective-permute-start.10 = (bf16[96,512]{1,0:T(8,128)(2,1)S(1)}, bf16[96,512]{1,0:T(8,128)(2,1)S(1)}, u32[]{:S(2)}, u32[]{:S(2)}) collective-permute-start(bf16[96,512]{1,0:T(8,128)(2,1)S(1)} %get-tuple-element.96), channel_id=1, source_target_pairs={{0,6},{1,7},{2,14},{3,15},{4,22},{5,23},{6,30},{7,31},{8,0},{9,1},... | collective-permute-start | bytes 294920 | tf_op jit(solution)/shard_map/ppermute | solution.py:45
  35.4 22.2 %collective-permute-start.16 = (bf16[3,96,512]{2,1,0:T(8,128)(2,1)S(1)}, bf16[3,96,512]{2,1,0:T(8,128)(2,1)S(1)}, u32[]{:S(2)}, u32[]{:S(2)}) collective-permute-start(bf16[3,96,512]{2,1,0:T(8,128)(2,1)S(1)} %get-tuple-element.104), channel_id=1, source_target_pairs={{0,4},{1,5},{2,6},{3,7},{4,0},{5,1},{6,2},{7,3},{8,12},{9,13},{10,... | collective-permute-start | bytes 884744 | tf_op jit(solution)/shard_map/ppermute | solution.py:30
  43.2 23.7 %collective-permute-start.17 = (bf16[3,96,512]{2,1,0:T(8,128)(2,1)S(1)}, bf16[3,96,512]{2,1,0:T(8,128)(2,1)S(1)}, u32[]{:S(2)}, u32[]{:S(2)}) collective-permute-start(bf16[3,96,512]{2,1,0:T(8,128)(2,1)S(1)} %get-tuple-element.104), channel_id=1, source_target_pairs={{0,6},{1,7},{2,0},{3,1},{4,2},{5,3},{6,4},{7,5},{8,14},{9,15},{10,... | collective-permute-start | bytes 884744 | tf_op jit(solution)/shard_map/ppermute | solution.py:30
  45.2 21.9 %collective-permute-start.28 = (bf16[1,4,96,512]{3,2,0,1:T(8,128)(2,1)S(1)}, bf16[1,4,96,512]{3,2,0,1:T(8,128)(2,1)S(1)}, u32[]{:S(2)}, u32[]{:S(2)}) collective-permute-start(bf16[1,4,96,512]{3,2,0,1:T(8,128)(2,1)S(1)} %pad_maximum_fusion.33), channel_id=1, source_target_pairs={{0,1},{1,0},{2,3},{3,2},{4,5},{5,4},{6,7},{7,6},{8,9},{9,8},{10,11... | collective-permute-start | bytes 1179656 | tf_op jit(solution)/shard_map/ppermute | solution.py:35
  45.4 31.0 %collective-permute-start.11 = (bf16[4,96,512]{2,1,0:T(8,128)(2,1)S(1)}, bf16[4,96,512]{2,1,0:T(8,128)(2,1)S(1)}, u32[]{:S(2)}, u32[]{:S(2)}) collective-permute-start(bf16[4,96,512]{2,1,0:T(8,128)(2,1)S(1)} %get-tuple-element.90), channel_id=1, source_target_pairs={{0,2},{1,3},{2,4},{3,5},{4,6},{5,7},{6,0},{7,1},{8,10},{9,11},{10,... | collective-permute-start | bytes 1179656 | tf_op jit(solution)/shard_map/ppermute | solution.py:30
  55.9 33.4 %collective-permute-start.12 = (bf16[4,96,512]{2,1,0:T(8,128)(2,1)S(1)}, bf16[4,96,512]{2,1,0:T(8,128)(2,1)S(1)}, u32[]{:S(2)}, u32[]{:S(2)}) collective-permute-start(bf16[4,96,512]{2,1,0:T(8,128)(2,1)S(1)} %get-tuple-element.90), channel_id=1, source_target_pairs={{0,4},{1,5},{2,6},{3,7},{4,0},{5,1},{6,2},{7,3},{8,12},{9,13},{10,... | collective-permute-start | bytes 1179656 | tf_op jit(solution)/shard_map/ppermute | solution.py:30
  57.7 31.6 %collective-permute-start.13 = (bf16[4,96,512]{2,1,0:T(8,128)(2,1)S(1)}, bf16[4,96,512]{2,1,0:T(8,128)(2,1)S(1)}, u32[]{:S(2)}, u32[]{:S(2)}) collective-permute-start(bf16[4,96,512]{2,1,0:T(8,128)(2,1)S(1)} %get-tuple-element.90), channel_id=1, source_target_pairs={{0,6},{1,7},{2,0},{3,1},{4,2},{5,3},{6,4},{7,5},{8,14},{9,15},{10,... | collective-permute-start | bytes 1179656 | tf_op jit(solution)/shard_map/ppermute | solution.py:30
  67.0 22.5 %collective-permute-start.18 = (bf16[3,4,96,512]{3,2,0,1:T(8,128)(2,1)S(1)}, bf16[3,4,96,512]{3,2,0,1:T(8,128)(2,1)S(1)}, u32[]{:S(2)}, u32[]{:S(2)}) collective-permute-start(bf16[3,4,96,512]{3,2,0,1:T(8,128)(2,1)S(1)} %pad_maximum_fusion.4), channel_id=1, source_target_pairs={{0,1},{1,0},{2,3},{3,2},{4,5},{5,4},{6,7},{7,6},{8,9},{9,8},{10,11... | collective-permute-start | bytes 3538952 | tf_op jit(solution)/shard_map/ppermute | solution.py:35
  69.1 40.7 %collective-permute-start.29 = (bf16[384,2048]{1,0:T(8,128)(2,1)S(1)}, bf16[384,2048]{1,0:T(8,128)(2,1)S(1)}, u32[]{:S(2)}, u32[]{:S(2)}) collective-permute-start(bf16[384,2048]{1,0:T(8,128)(2,1)S(1)} %convolution_convert_fusion.1), channel_id=1, source_target_pairs={{0,8},{8,0},{16,24},{24,16},{1,9},{9,1},{17,25},{25,17},{2,10},{10... | collective-permute-start | bytes 4718600 | tf_op jit(solution)/shard_map/ppermute | solution.py:13
  76.4 46.5 %collective-permute-start.31 = (bf16[384,2048]{1,0:T(8,128)(2,1)S(1)}, bf16[384,2048]{1,0:T(8,128)(2,1)S(1)}, u32[]{:S(2)}, u32[]{:S(2)}) collective-permute-start(bf16[384,2048]{1,0:T(8,128)(2,1)S(1)} %convolution_convert_fusion), channel_id=1, source_target_pairs={{0,16},{8,24},{16,0},{24,8},{1,17},{9,25},{17,1},{25,9},{2,18},{10... | collective-permute-start | bytes 4718600 | tf_op jit(solution)/shard_map/ppermute | solution.py:13
  89.5 37.4 %collective-permute-start.14 = (bf16[4,4,96,512]{3,2,0,1:T(8,128)(2,1)S(1)}, bf16[4,4,96,512]{3,2,0,1:T(8,128)(2,1)S(1)}, u32[]{:S(2)}, u32[]{:S(2)}) collective-permute-start(bf16[4,4,96,512]{3,2,0,1:T(8,128)(2,1)S(1)} %pad_maximum_fusion), channel_id=1, source_target_pairs={{0,1},{1,0},{2,3},{3,2},{4,5},{5,4},{6,7},{7,6},{8,9},{9,8},{10,11... | collective-permute-start | bytes 4718600 | tf_op jit(solution)/shard_map/ppermute | solution.py:35
  89.8 120.2 %copy-start.5 = (bf16[1,4,96,512]{3,2,0,1:T(8,128)(2,1)}, bf16[1,4,96,512]{3,2,0,1:T(8,128)(2,1)S(1)}, u32[]{:S(2)}) copy-start(bf16[1,4,96,512]{3,2,0,1:T(8,128)(2,1)S(1)} %get-tuple-element.58) | copy-start | bytes 1179652
  91.6 65.1 %collective-permute-start.20 = (bf16[384,2048]{1,0:T(8,128)(2,1)S(1)}, bf16[384,2048]{1,0:T(8,128)(2,1)S(1)}, u32[]{:S(2)}, u32[]{:S(2)}) collective-permute-start(bf16[384,2048]{1,0:T(8,128)(2,1)S(1)} %convolution_convert_fusion.2), channel_id=1, source_target_pairs={{0,16},{8,24},{16,0},{24,8},{1,17},{9,25},{17,1},{25,9},{2,18},{10... | collective-permute-start | bytes 4718600 | tf_op jit(solution)/shard_map/ppermute | solution.py:13
  99.7 56.9 %collective-permute-start.19 = (bf16[384,2048]{1,0:T(8,128)(2,1)S(1)}, bf16[384,2048]{1,0:T(8,128)(2,1)S(1)}, u32[]{:S(2)}, u32[]{:S(2)}) collective-permute-start(bf16[384,2048]{1,0:T(8,128)(2,1)S(1)} %convolution_convert_fusion.3), channel_id=1, source_target_pairs={{0,8},{8,0},{16,24},{24,16},{1,9},{9,1},{17,25},{25,17},{2,10},{10... | collective-permute-start | bytes 4718600 | tf_op jit(solution)/shard_map/ppermute | solution.py:13
  111.6 98.3 %collective-permute-start.30 = (bf16[384,2048]{1,0:T(8,128)(2,1)S(1)}, bf16[384,2048]{1,0:T(8,128)(2,1)S(1)}, u32[]{:S(2)}, u32[]{:S(2)}) collective-permute-start(bf16[384,2048]{1,0:T(8,128)(2,1)S(1)} %add_convert_fusion.1), channel_id=1, source_target_pairs={{0,16},{8,24},{16,0},{24,8},{1,17},{9,25},{17,1},{25,9},{2,18},{10... | collective-permute-start | bytes 4718600 | tf_op jit(solution)/shard_map/ppermute | solution.py:13
  124.8 85.2 %collective-permute-start.32 = (bf16[384,2048]{1,0:T(8,128)(2,1)S(1)}, bf16[384,2048]{1,0:T(8,128)(2,1)S(1)}, u32[]{:S(2)}, u32[]{:S(2)}) collective-permute-start(bf16[384,2048]{1,0:T(8,128)(2,1)S(1)} %add_convert_fusion), channel_id=1, source_target_pairs={{0,8},{8,0},{16,24},{24,16},{1,9},{9,1},{17,25},{25,17},{2,10},{10... | collective-permute-start | bytes 4718600 | tf_op jit(solution)/shard_map/ppermute | solution.py:13
  156.7 50.1 %collective-permute-start.23 = (bf16[192,2048]{1,0:T(8,128)(2,1)S(1)}, bf16[192,2048]{1,0:T(8,128)(2,1)S(1)}, u32[]{:S(2)}, u32[]{:S(2)}) collective-permute-start(bf16[192,2048]{1,0:T(8,128)(2,1)S(1)} %convolution_convert_fusion.6), channel_id=1, source_target_pairs={{0,16},{8,24},{16,0},{24,8},{1,17},{9,25},{17,1},{25,9},{2,18},{10... | collective-permute-start | bytes 2359304 | tf_op jit(solution)/shard_map/ppermute | solution.py:13
  158.7 60.1 %collective-permute-start = (s32[1,4]{1,0:T(1,128)}, s32[1,4]{1,0:T(1,128)}, u32[]{:S(2)}, u32[]{:S(2)}) collective-permute-start(s32[1,4]{1,0:T(1,128)} %param.8), channel_id=1, source_target_pairs={{0,8},{8,0},{16,24},{24,16},{1,9},{9,1},{17,25},{25,17},{2,10},{10... | collective-permute-start | bytes 56 | tf_op jit(solution)/shard_map/ppermute | solution.py:13
  161.6 103.8 %collective-permute-start.21 = (bf16[192,2048]{1,0:T(8,128)(2,1)}, bf16[192,2048]{1,0:T(8,128)(2,1)S(1)}, u32[]{:S(2)}, u32[]{:S(2)}) collective-permute-start(bf16[192,2048]{1,0:T(8,128)(2,1)} %convolution_convert_fusion.7), channel_id=1, source_target_pairs={{0,8},{8,0},{16,24},{24,16},{1,9},{9,1},{17,25},{25,17},{2,10},{10... | collective-permute-start | bytes 2359304 | tf_op jit(solution)/shard_map/ppermute | solution.py:13
  209.2 61.5 %collective-permute-start.24 = (bf16[192,2048]{1,0:T(8,128)(2,1)}, bf16[192,2048]{1,0:T(8,128)(2,1)}, u32[]{:S(2)}, u32[]{:S(2)}) collective-permute-start(bf16[192,2048]{1,0:T(8,128)(2,1)} %add_convert_fusion.7), channel_id=1, source_target_pairs={{0,8},{8,0},{16,24},{24,16},{1,9},{9,1},{17,25},{25,17},{2,10},{10... | collective-permute-start | bytes 2359304 | tf_op jit(solution)/shard_map/ppermute | solution.py:13
  214.6 85.4 %collective-permute-start.33 = (bf16[384,2048]{1,0:T(8,128)(2,1)}, bf16[384,2048]{1,0:T(8,128)(2,1)}, u32[]{:S(2)}, u32[]{:S(2)}) collective-permute-start(bf16[384,2048]{1,0:T(8,128)(2,1)} %get-tuple-element.113), channel_id=1, source_target_pairs={{0,8},{8,0},{16,24},{24,16},{1,9},{9,1},{17,25},{25,17},{2,10},{10... | collective-permute-start | bytes 4718600 | tf_op jit(solution)/shard_map/ppermute | solution.py:13
  215.8 84.2 %collective-permute-start.34 = (bf16[384,2048]{1,0:T(8,128)(2,1)}, bf16[384,2048]{1,0:T(8,128)(2,1)}, u32[]{:S(2)}, u32[]{:S(2)}) collective-permute-start(bf16[384,2048]{1,0:T(8,128)(2,1)} %get-tuple-element.113), channel_id=1, source_target_pairs={{0,16},{8,24},{16,0},{24,8},{1,17},{9,25},{17,1},{25,9},{2,18},{10... | collective-permute-start | bytes 4718600 | tf_op jit(solution)/shard_map/ppermute | solution.py:13
  218.9 32.6 %collective-permute-start.1 = (s32[1,4]{1,0:T(1,128)}, s32[1,4]{1,0:T(1,128)S(1)}, u32[]{:S(2)}, u32[]{:S(2)}) collective-permute-start(s32[1,4]{1,0:T(1,128)} %param.8), channel_id=1, source_target_pairs={{0,16},{8,24},{16,0},{24,8},{1,17},{9,25},{17,1},{25,9},{2,18},{10... | collective-permute-start | bytes 56 | tf_op jit(solution)/shard_map/ppermute | solution.py:13
  251.5 11.5 %collective-permute-start.2 = (s32[1,4]{1,0:T(1,128)}, s32[1,4]{1,0:T(1,128)S(1)}, u32[]{:S(2)}, u32[]{:S(2)}) collective-permute-start(s32[1,4]{1,0:T(1,128)} %param.8), channel_id=1, source_target_pairs={{0,24},{8,16},{16,8},{24,0},{1,25},{9,17},{17,9},{25,1},{2,26},{10... | collective-permute-start | bytes 56 | tf_op jit(solution)/shard_map/ppermute | solution.py:13
  264.3 39.8 %collective-permute-start.37 = (bf16[192,2048]{1,0:T(8,128)(2,1)}, bf16[192,2048]{1,0:T(8,128)(2,1)}, u32[]{:S(2)}, u32[]{:S(2)}) collective-permute-start(bf16[192,2048]{1,0:T(8,128)(2,1)} %convolution_convert_fusion.5), channel_id=1, source_target_pairs={{0,8},{8,0},{16,24},{24,16},{1,9},{9,1},{17,25},{25,17},{2,10},{10... | collective-permute-start | bytes 2359304 | tf_op jit(solution)/shard_map/ppermute | solution.py:13
  265.5 38.7 %collective-permute-start.38 = (bf16[192,2048]{1,0:T(8,128)(2,1)S(1)}, bf16[192,2048]{1,0:T(8,128)(2,1)}, u32[]{:S(2)}, u32[]{:S(2)}) collective-permute-start(bf16[192,2048]{1,0:T(8,128)(2,1)S(1)} %convolution_convert_fusion.4), channel_id=1, source_target_pairs={{0,16},{8,24},{16,0},{24,8},{1,17},{9,25},{17,1},{25,9},{2,18},{10... | collective-permute-start | bytes 2359304 | tf_op jit(solution)/shard_map/ppermute | solution.py:13
  270.6 29.4 %collective-permute-start.22 = (bf16[192,2048]{1,0:T(8,128)(2,1)}, bf16[192,2048]{1,0:T(8,128)(2,1)}, u32[]{:S(2)}, u32[]{:S(2)}) collective-permute-start(bf16[192,2048]{1,0:T(8,128)(2,1)} %add_convert_fusion.8), channel_id=1, source_target_pairs={{0,16},{8,24},{16,0},{24,8},{1,17},{9,25},{17,1},{25,9},{2,18},{10... | collective-permute-start | bytes 2359304 | tf_op jit(solution)/shard_map/ppermute | solution.py:13
  301.3 19.5 %collective-permute-start.35 = (bf16[192,2048]{1,0:T(8,128)(2,1)S(1)}, bf16[192,2048]{1,0:T(8,128)(2,1)S(1)}, u32[]{:S(2)}, u32[]{:S(2)}) collective-permute-start(bf16[192,2048]{1,0:T(8,128)(2,1)S(1)} %slice.176), channel_id=1, source_target_pairs={{0,8},{8,0},{16,24},{24,16},{1,9},{9,1},{17,25},{25,17},{2,10},{10... | collective-permute-start | bytes 2359304 | tf_op jit(solution)/shard_map/ppermute | solution.py:13
  303.2 20.5 %collective-permute-start.36 = (bf16[192,2048]{1,0:T(8,128)(2,1)S(1)}, bf16[192,2048]{1,0:T(8,128)(2,1)S(1)}, u32[]{:S(2)}, u32[]{:S(2)}) collective-permute-start(bf16[192,2048]{1,0:T(8,128)(2,1)S(1)} %slice.177), channel_id=1, source_target_pairs={{0,16},{8,24},{16,0},{24,8},{1,17},{9,25},{17,1},{25,9},{2,18},{10... | collective-permute-start | bytes 2359304 | tf_op jit(solution)/shard_map/ppermute | solution.py:13
  315.2 42.3 %collective-permute-start.44 = (bf16[384,2048]{1,0:T(8,128)(2,1)}, bf16[384,2048]{1,0:T(8,128)(2,1)}, u32[]{:S(2)}, u32[]{:S(2)}) collective-permute-start(bf16[384,2048]{1,0:T(8,128)(2,1)} %get-tuple-element.43), channel_id=1, source_target_pairs={{0,16},{8,24},{16,0},{24,8},{1,17},{9,25},{17,1},{25,9},{2,18},{10... | collective-permute-start | bytes 4718600 | tf_op jit(solution)/shard_map/ppermute | solution.py:13
  316.4 48.0 %collective-permute-start.43 = (bf16[384,2048]{1,0:T(8,128)(2,1)}, bf16[384,2048]{1,0:T(8,128)(2,1)}, u32[]{:S(2)}, u32[]{:S(2)}) collective-permute-start(bf16[384,2048]{1,0:T(8,128)(2,1)} %get-tuple-element.43), channel_id=1, source_target_pairs={{0,8},{8,0},{16,24},{24,16},{1,9},{9,1},{17,25},{25,17},{2,10},{10... | collective-permute-start | bytes 4718600 | tf_op jit(solution)/shard_map/ppermute | solution.py:13
  331.0 6.6 %collective-permute-start.39 = (bf16[1,384,512]{2,1,0:T(8,128)(2,1)}, bf16[1,384,512]{2,1,0:T(8,128)(2,1)}, u32[]{:S(2)}, u32[]{:S(2)}) collective-permute-start(bf16[1,384,512]{2,1,0:T(8,128)(2,1)} %dynamic-slice_bitcast_fusion.1), channel_id=1, source_target_pairs={{0,1},{1,0},{2,3},{3,2},{4,5},{5,4},{6,7},{7,6},{8,9},{9,8},{10,11... | collective-permute-start | bytes 1179656 | tf_op jit(solution)/shard_map/ppermute | solution.py:35
  332.4 55.8 %collective-permute-start.46 = (bf16[384,2048]{1,0:T(8,128)(2,1)}, bf16[384,2048]{1,0:T(8,128)(2,1)}, u32[]{:S(2)}, u32[]{:S(2)}) collective-permute-start(bf16[384,2048]{1,0:T(8,128)(2,1)} %copy-done.41), channel_id=1, source_target_pairs={{0,16},{8,24},{16,0},{24,8},{1,17},{9,25},{17,1},{25,9},{2,18},{10... | collective-permute-start | bytes 4718600 | tf_op jit(solution)/shard_map/ppermute | solution.py:13
  336.2 58.5 %collective-permute-start.45 = (bf16[384,2048]{1,0:T(8,128)(2,1)}, bf16[384,2048]{1,0:T(8,128)(2,1)S(1)}, u32[]{:S(2)}, u32[]{:S(2)}) collective-permute-start(bf16[384,2048]{1,0:T(8,128)(2,1)} %copy-done.41), channel_id=1, source_target_pairs={{0,8},{8,0},{16,24},{24,16},{1,9},{9,1},{17,25},{25,17},{2,10},{10... | collective-permute-start | bytes 4718600 | tf_op jit(solution)/shard_map/ppermute | solution.py:13
  339.5 59.8 %collective-permute-start.40 = (bf16[1,384,128]{2,1,0:T(8,128)(2,1)S(1)}, bf16[1,384,128]{2,1,0:T(8,128)(2,1)S(1)}, u32[]{:S(2)}, u32[]{:S(2)}) collective-permute-start(bf16[1,384,128]{2,1,0:T(8,128)(2,1)S(1)} %get-tuple-element.79), channel_id=1, source_target_pairs={{0,2},{1,3},{2,4},{3,5},{4,6},{5,7},{6,0},{7,1},{8,10},{9,11},{10,... | collective-permute-start | bytes 294920 | tf_op jit(solution)/shard_map/ppermute | solution.py:30
  357.5 43.1 %collective-permute-start.42 = (bf16[1,384,128]{2,1,0:T(8,128)(2,1)S(1)}, bf16[1,384,128]{2,1,0:T(8,128)(2,1)S(1)}, u32[]{:S(2)}, u32[]{:S(2)}) collective-permute-start(bf16[1,384,128]{2,1,0:T(8,128)(2,1)S(1)} %get-tuple-element.77), channel_id=1, source_target_pairs={{0,6},{1,7},{2,0},{3,1},{4,2},{5,3},{6,4},{7,5},{8,14},{9,15},{10,... | collective-permute-start | bytes 294920 | tf_op jit(solution)/shard_map/ppermute | solution.py:30
  364.4 51.6 %collective-permute-start.51 = (bf16[192,2048]{1,0:T(8,128)(2,1)}, bf16[192,2048]{1,0:T(8,128)(2,1)}, u32[]{:S(2)}, u32[]{:S(2)}) collective-permute-start(bf16[192,2048]{1,0:T(8,128)(2,1)} %slice.238), channel_id=1, source_target_pairs={{0,8},{8,0},{16,24},{24,16},{1,9},{9,1},{17,25},{25,17},{2,10},{10... | collective-permute-start | bytes 2359304 | tf_op jit(solution)/shard_map/ppermute | solution.py:13
  388.2 28.9 %collective-permute-start.52 = (bf16[192,2048]{1,0:T(8,128)(2,1)}, bf16[192,2048]{1,0:T(8,128)(2,1)}, u32[]{:S(2)}, u32[]{:S(2)}) collective-permute-start(bf16[192,2048]{1,0:T(8,128)(2,1)} %slice.239), channel_id=1, source_target_pairs={{0,16},{8,24},{16,0},{24,8},{1,17},{9,25},{17,1},{25,9},{2,18},{10... | collective-permute-start | bytes 2359304 | tf_op jit(solution)/shard_map/ppermute | solution.py:13
  394.7 24.6 %collective-permute-start.53 = (bf16[192,2048]{1,0:T(8,128)(2,1)}, bf16[192,2048]{1,0:T(8,128)(2,1)}, u32[]{:S(2)}, u32[]{:S(2)}) collective-permute-start(bf16[192,2048]{1,0:T(8,128)(2,1)} %slice.240), channel_id=1, source_target_pairs={{0,8},{8,0},{16,24},{24,16},{1,9},{9,1},{17,25},{25,17},{2,10},{10... | collective-permute-start | bytes 2359304 | tf_op jit(solution)/shard_map/ppermute | solution.py:13
  399.4 21.3 %collective-permute-start.54 = (bf16[192,2048]{1,0:T(8,128)(2,1)}, bf16[192,2048]{1,0:T(8,128)(2,1)}, u32[]{:S(2)}, u32[]{:S(2)}) collective-permute-start(bf16[192,2048]{1,0:T(8,128)(2,1)} %slice.241), channel_id=1, source_target_pairs={{0,16},{8,24},{16,0},{24,8},{1,17},{9,25},{17,1},{25,9},{2,18},{10... | collective-permute-start | bytes 2359304 | tf_op jit(solution)/shard_map/ppermute | solution.py:13
  401.3 20.9 %collective-permute-start.47 = (bf16[2,384,512]{2,1,0:T(8,128)(2,1)S(1)}, bf16[2,384,512]{2,1,0:T(8,128)(2,1)}, u32[]{:S(2)}, u32[]{:S(2)}) collective-permute-start(bf16[2,384,512]{2,1,0:T(8,128)(2,1)S(1)} %fusion.51), channel_id=1, source_target_pairs={{0,1},{1,0},{2,3},{3,2},{4,5},{5,4},{6,7},{7,6},{8,9},{9,8},{10,11... | collective-permute-start | bytes 2359304 | tf_op jit(solution)/shard_map/ppermute | solution.py:35
  416.0 18.7 %collective-permute-start.41 = (bf16[1,384,128]{2,1,0:T(8,128)(2,1)}, bf16[1,384,128]{2,1,0:T(8,128)(2,1)S(1)}, u32[]{:S(2)}, u32[]{:S(2)}) collective-permute-start(bf16[1,384,128]{2,1,0:T(8,128)(2,1)} %get-tuple-element.78), channel_id=1, source_target_pairs={{0,4},{1,5},{2,6},{3,7},{4,0},{5,1},{6,2},{7,3},{8,12},{9,13},{10,... | collective-permute-start | bytes 294920 | tf_op jit(solution)/shard_map/ppermute | solution.py:30
  423.9 16.9 %collective-permute-start.49 = (bf16[2,384,128]{2,1,0:T(8,128)(2,1)S(1)}, bf16[2,384,128]{2,1,0:T(8,128)(2,1)S(1)}, u32[]{:S(2)}, u32[]{:S(2)}) collective-permute-start(bf16[2,384,128]{2,1,0:T(8,128)(2,1)S(1)} %get-tuple-element.69), channel_id=1, source_target_pairs={{0,4},{1,5},{2,6},{3,7},{4,0},{5,1},{6,2},{7,3},{8,12},{9,13},{10,... | collective-permute-start | bytes 589832 | tf_op jit(solution)/shard_map/ppermute | solution.py:30
  425.1 15.1 %collective-permute-start.48 = (bf16[2,384,128]{2,1,0:T(8,128)(2,1)S(1)}, bf16[2,384,128]{2,1,0:T(8,128)(2,1)S(1)}, u32[]{:S(2)}, u32[]{:S(2)}) collective-permute-start(bf16[2,384,128]{2,1,0:T(8,128)(2,1)S(1)} %get-tuple-element.70), channel_id=1, source_target_pairs={{0,2},{1,3},{2,4},{3,5},{4,6},{5,7},{6,0},{7,1},{8,10},{9,11},{10,... | collective-permute-start | bytes 589832 | tf_op jit(solution)/shard_map/ppermute | solution.py:30
  429.2 11.7 %collective-permute-start.50 = (bf16[2,384,128]{2,1,0:T(8,128)(2,1)S(1)}, bf16[2,384,128]{2,1,0:T(8,128)(2,1)S(1)}, u32[]{:S(2)}, u32[]{:S(2)}) collective-permute-start(bf16[2,384,128]{2,1,0:T(8,128)(2,1)S(1)} %get-tuple-element.68), channel_id=1, source_target_pairs={{0,6},{1,7},{2,0},{3,1},{4,2},{5,3},{6,4},{7,5},{8,14},{9,15},{10,... | collective-permute-start | bytes 589832 | tf_op jit(solution)/shard_map/ppermute | solution.py:30
  434.6 6.3 %collective-permute-start.55 = (bf16[1,384,512]{2,1,0:T(8,128)(2,1)S(1)}, bf16[1,384,512]{2,1,0:T(8,128)(2,1)S(1)}, u32[]{:S(2)}, u32[]{:S(2)}) collective-permute-start(bf16[1,384,512]{2,1,0:T(8,128)(2,1)S(1)} %dynamic-slice_bitcast_fusion), channel_id=1, source_target_pairs={{0,1},{1,0},{2,3},{3,2},{4,5},{5,4},{6,7},{7,6},{8,9},{9,8},{10,11... | collective-permute-start | bytes 1179656 | tf_op jit(solution)/shard_map/ppermute | solution.py:35
  441.1 12.5 %collective-permute-start.57 = (bf16[1,384,128]{2,1,0:T(8,128)(2,1)S(1)}, bf16[1,384,128]{2,1,0:T(8,128)(2,1)S(1)}, u32[]{:S(2)}, u32[]{:S(2)}) collective-permute-start(bf16[1,384,128]{2,1,0:T(8,128)(2,1)S(1)} %get-tuple-element.82), channel_id=1, source_target_pairs={{0,4},{1,5},{2,6},{3,7},{4,0},{5,1},{6,2},{7,3},{8,12},{9,13},{10,... | collective-permute-start | bytes 294920 | tf_op jit(solution)/shard_map/ppermute | solution.py:30
  445.4 7.3 %collective-permute-start.56 = (bf16[1,384,128]{2,1,0:T(8,128)(2,1)S(1)}, bf16[1,384,128]{2,1,0:T(8,128)(2,1)S(1)}, u32[]{:S(2)}, u32[]{:S(2)}) collective-permute-start(bf16[1,384,128]{2,1,0:T(8,128)(2,1)S(1)} %get-tuple-element.83), channel_id=1, source_target_pairs={{0,2},{1,3},{2,4},{3,5},{4,6},{5,7},{6,0},{7,1},{8,10},{9,11},{10,... | collective-permute-start | bytes 294920 | tf_op jit(solution)/shard_map/ppermute | solution.py:30
  445.4 8.3 %collective-permute-start.58 = (bf16[1,384,128]{2,1,0:T(8,128)(2,1)S(1)}, bf16[1,384,128]{2,1,0:T(8,128)(2,1)S(1)}, u32[]{:S(2)}, u32[]{:S(2)}) collective-permute-start(bf16[1,384,128]{2,1,0:T(8,128)(2,1)S(1)} %get-tuple-element.81), channel_id=1, source_target_pairs={{0,6},{1,7},{2,0},{3,1},{4,2},{5,3},{6,4},{7,5},{8,14},{9,15},{10,... | collective-permute-start | bytes 294920 | tf_op jit(solution)/shard_map/ppermute | solution.py:30
  456.5 16.1 %all-to-all-start = ((bf16[4,576,128]{2,1,0:T(8,128)(2,1)}), bf16[4,576,128]{2,1,0:T(8,128)(2,1)S(1)}, u32[]{:S(2)}, u32[]{:S(2)}) async-start(bf16[4,576,128]{2,1,0:T(8,128)(2,1)} %fusion.61), calls=%async_computation | async-start | bytes 1179648 | tf_op jit(solution)/shard_map/all_to_all | solution.py:150
  472.6 15.9 %collective-permute-start.59 = (bf16[576,128]{1,0:T(8,128)(2,1)S(1)}, bf16[576,128]{1,0:T(8,128)(2,1)S(1)}, u32[]{:S(2)}, u32[]{:S(2)}) collective-permute-start(bf16[576,128]{1,0:T(8,128)(2,1)S(1)} %get-tuple-element.76), channel_id=1, source_target_pairs={{0,6},{1,7},{2,0},{3,1},{4,2},{5,3},{6,4},{7,5},{8,14},{9,15},{10,... | collective-permute-start | bytes 442376 | tf_op jit(solution)/shard_map/ppermute | solution.py:30
  475.2 13.7 %collective-permute-start.60 = (bf16[576,128]{1,0:T(8,128)(2,1)S(1)}, bf16[576,128]{1,0:T(8,128)(2,1)S(1)}, u32[]{:S(2)}, u32[]{:S(2)}) collective-permute-start(bf16[576,128]{1,0:T(8,128)(2,1)S(1)} %get-tuple-element.75), channel_id=1, source_target_pairs={{0,4},{1,5},{2,6},{3,7},{4,0},{5,1},{6,2},{7,3},{8,12},{9,13},{10,... | collective-permute-start | bytes 442376 | tf_op jit(solution)/shard_map/ppermute | solution.py:30
  475.8 13.1 %collective-permute-start.61 = (bf16[576,128]{1,0:T(8,128)(2,1)S(1)}, bf16[576,128]{1,0:T(8,128)(2,1)S(1)}, u32[]{:S(2)}, u32[]{:S(2)}) collective-permute-start(bf16[576,128]{1,0:T(8,128)(2,1)S(1)} %get-tuple-element.74), channel_id=1, source_target_pairs={{0,2},{1,3},{2,4},{3,5},{4,6},{5,7},{6,0},{7,1},{8,10},{9,11},{10,... | collective-permute-start | bytes 442376 | tf_op jit(solution)/shard_map/ppermute | solution.py:30
  (42 other events, 924.2 us)

commit v2 on v1

--- a/solution.py
+++ b/solution.py
@@ -221,6 +221,12 @@
     hidden = low(silu_gate * up_act)
     hidden1, hidden2 = swap_x(hidden), swap_y(hidden)
 
+    *in_blocks, _ = fence(in0, in1, in2, in3, hidden)
+    *cot_blocks, _ = fence(cot0, cot1, cot2, cot3, hidden)
+    rows_in = jnp.concatenate(in_blocks, axis=0)
+    rows_cot = jnp.concatenate(cot_blocks, axis=0)
+    rows_in, rows_cot = fence(rows_in, rows_cot)
+
     h2a_came = swap_y(low(plus(h2a, h3a_came)))
     h1b_came = swap_x(low(plus(h1b, h3b_came)))
 
@@ -243,8 +249,6 @@
     gate1, gate2 = swap_x(gate0), swap_y(gate0)
     terms0 = input_terms(up0, gate0)
     terms0 = sum_over_tensor(grid, terms0[None])
-    rows_in = jnp.concatenate([in0, in1, in2, in3], axis=0)
-    rows_cot = jnp.concatenate([cot0, cot1, cot2, cot3], axis=0)
     all_hidden = jnp.concatenate([hidden, hidden1, hidden2, hidden3], axis=0)
     grad_down = low(contract_rows(all_hidden, rows_cot))
 

time: 494 us -> 487 us (0.986)
  waiting for transfers between devices: 198 us -> 231 us
  matrix products: 101 us -> 81.1 us
  starting transfers between devices: 149 us -> 141 us
  local copies, waits for them, and re-layouts: 22.4 us -> 14.5 us
    ppermute x21, waiting for transfers between devices: 14.1 us -> 47.7 us  [shift_line(): return lax.ppermute(values, 'tensor', pairs)]
    ppermute x27, starting transfers between devices: 61.3 us -> 42.2 us  [swap(): return lax.ppermute(values, 'fsdp', [(i, i ^ offset) for i in range(size)])]
    dot_general x15, matrix products: 48.3 us -> 35.4 us  [matmul_t(): lax.dot_general(left_side, right_side, (((1,), (1,)), ((), ())), preferre...]
    ppermute x21, starting transfers between devices: 61.7 us -> 72.6 us  [shift_line(): return lax.ppermute(values, 'tensor', pairs)]
    dot_general x3, matrix products: 35.5 us -> 28.9 us  [contract_rows(): lax.dot_general(left_side, right_side, (((0,), (0,)), ((), ())), preferre...]
    unnamed x86 -> x54, local copies, waits for them, and re-layouts: 2.04 us -> 8.49 us
  transfers between devices with their start and end apart: 63 -> 63, of which waited for: 23 -> 20; matrix products, arithmetic and copies ran while one was open for 27% -> 19% of each run, Pallas kernels for 0% -> 0%
where the time goes in v2:
time: 487 us; the launch traced here: 483 us
  waiting for transfers between devices  231 us (47%)
  starting transfers between devices  141 us (29%)
  matrix products  81.1 us (17%)
  local copies, waits for them, and re-layouts  14.5 us (3%)
  other arithmetic  13 us (3%)
    ppermute x27, waiting for transfers between devices, swap(): return lax.ppermute(values, 'fsdp', [(i, i ^ offset) for i in range(size)])  182 us
    ppermute x21, starting transfers between devices, shift_line(): return lax.ppermute(values, 'tensor', pairs)  72.6 us
    ppermute x21, waiting for transfers between devices, shift_line(): return lax.ppermute(values, 'tensor', pairs)  47.7 us
    ppermute x27, starting transfers between devices, swap(): return lax.ppermute(values, 'fsdp', [(i, i ^ offset) for i in range(size)])  42.2 us
    dot_general x15, matrix products, matmul_t(): lax.dot_general(left_side, right_side, (((1,), (1,)), ((), ())), preferre...  35.4 us
    dot_general x3, matrix products, contract_rows(): lax.dot_general(left_side, right_side, (((0,), (0,)), ((), ())), preferre...  28.9 us
    ppermute x8, starting transfers between devices, across(): return lax.ppermute(values, ('fsdp', 'tensor'), pairs)  22.2 us
    dot_general x8, matrix products, matmul(): return jnp.dot(left_side, right_side, preferred_element_type=jnp.float32)  16.9 us
  transfers between devices with their start and end apart: 63, of which 20 were waited for; matrix products, arithmetic and copies ran while one was open for 19% of the time, Pallas kernels for 0%

profile of v2, /device:TPU:0, one launch (start us, length us, event | category | flops | bytes accessed | tf_op | source)
XLA Modules:
  0.0 483.4 jit_solution(11607700849930912280)
XLA Ops:
  0.6 3.0 collective-permute-start
  7.0 4.7 collective-permute-start.4
  12.1 3.5 collective-permute-start.5
  15.6 2.3 collective-permute-start.6
  22.4 6.3 %collective-permute-start.8 = (bf16[96,512]{1,0:T(8,128)(2,1)S(1)}, bf16[96,512]{1,0:T(8,128)(2,1)S(1)}, u32[]{:S(2)}, u32[]{:S(2)}) collective-permute-start(bf16[96,512]{1,0:T(8,128)(2,1)S(1)} %get-tuple-element.118), channel_id=1, source_target_pairs={{0,2},{1,3},{2,10},{3,11},{4,18},{5,19},{6,26},{7,27},{8,4},{9,5},... | collective-permute-start | bytes 294920 | tf_op jit(solution)/shard_map/ppermute | solution.py:45
  30.2 2.5 collective-permute-start.10
  34.8 2.7 collective-permute-start.27
  38.6 3.2 collective-permute-start.16
  42.0 5.1 %collective-permute-start.17 = (bf16[3,96,512]{2,1,0:T(8,128)(2,1)}, bf16[3,96,512]{2,1,0:T(8,128)(2,1)}, u32[]{:S(2)}, u32[]{:S(2)}) collective-permute-start(bf16[3,96,512]{2,1,0:T(8,128)(2,1)} %get-tuple-element.124), channel_id=1, source_target_pairs={{0,6},{1,7},{2,0},{3,1},{4,2},{5,3},{6,4},{7,5},{8,14},{9,15},{10,... | collective-permute-start | bytes 884744 | tf_op jit(solution)/shard_map/ppermute | solution.py:30
  47.1 8.0 %collective-permute-done.26 = bf16[1,96,512]{2,1,0:T(8,128)(2,1)S(1)} collective-permute-done((bf16[1,96,512]{2,1,0:T(8,128)(2,1)S(1)}, bf16[1,96,512]{2,1,0:T(8,128)(2,1)S(1)}, u32[]{:S(2)}, u32[]{:S(2)}) %collective-permute-start.26) | collective-permute-done | bytes 98336 | tf_op jit(solution)/shard_map/ppermute | solution.py:30
  55.1 2.8 collective-permute-start.12
  58.0 3.5 collective-permute-start.13
  61.6 20.0 %collective-permute-done.16 = bf16[3,96,512]{2,1,0:T(8,128)(2,1)S(1)} collective-permute-done((bf16[3,96,512]{2,1,0:T(8,128)(2,1)}, bf16[3,96,512]{2,1,0:T(8,128)(2,1)S(1)}, u32[]{:S(2)}, u32[]{:S(2)}) %collective-permute-start.16) | collective-permute-done | bytes 294944 | tf_op jit(solution)/shard_map/ppermute | solution.py:30
  84.4 12.0 %collective-permute-done.12 = bf16[4,96,512]{2,1,0:T(8,128)(2,1)S(1)} collective-permute-done((bf16[4,96,512]{2,1,0:T(8,128)(2,1)S(1)}, bf16[4,96,512]{2,1,0:T(8,128)(2,1)S(1)}, u32[]{:S(2)}, u32[]{:S(2)}) %collective-permute-start.12) | collective-permute-done | bytes 393248 | tf_op jit(solution)/shard_map/ppermute | solution.py:30
  96.7 1.8 copy-done.12
  100.3 2.5 collective-permute-start.29
  104.6 2.3 collective-permute-start.31
  107.1 1.8 convolution_convert_fusion.2
  114.3 23.7 %collective-permute-done.29 = bf16[384,2048]{1,0:T(8,128)(2,1)S(1)} collective-permute-done((bf16[384,2048]{1,0:T(8,128)(2,1)S(1)}, bf16[384,2048]{1,0:T(8,128)(2,1)S(1)}, u32[]{:S(2)}, u32[]{:S(2)}) %collective-permute-start.29) | collective-permute-done | bytes 1572896 | tf_op jit(solution)/shard_map/ppermute | solution.py:13
  138.1 1.8 add_convert_fusion.1
  139.9 4.0 collective-permute-start.30
  146.0 1.8 copy-done
  149.4 1.9 convolution_convert_fusion.7
  154.4 21.5 %collective-permute-done.20 = bf16[384,2048]{1,0:T(8,128)(2,1)S(1)} collective-permute-done((bf16[384,2048]{1,0:T(8,128)(2,1)S(1)}, bf16[384,2048]{1,0:T(8,128)(2,1)S(1)}, u32[]{:S(2)}, u32[]{:S(2)}) %collective-permute-start.20) | collective-permute-done | bytes 1572896 | tf_op jit(solution)/shard_map/ppermute | solution.py:13
  175.9 2.0 collective-permute-start.23
  179.6 30.0 %collective-permute-done.30 = bf16[384,2048]{1,0:T(8,128)(2,1)S(1)} collective-permute-done((bf16[384,2048]{1,0:T(8,128)(2,1)S(1)}, bf16[384,2048]{1,0:T(8,128)(2,1)S(1)}, u32[]{:S(2)}, u32[]{:S(2)}) %collective-permute-start.30) | collective-permute-done | bytes 1572896 | tf_op jit(solution)/shard_map/ppermute | solution.py:13
  209.6 4.3 multiply_convert_fusion.2
  215.7 2.0 collective-permute-start.34
  217.7 8.7 %collective-permute-done.23 = bf16[192,2048]{1,0:T(8,128)(2,1)S(1)} collective-permute-done((bf16[192,2048]{1,0:T(8,128)(2,1)S(1)}, bf16[192,2048]{1,0:T(8,128)(2,1)S(1)}, u32[]{:S(2)}, u32[]{:S(2)}) %collective-permute-start.23) | collective-permute-done | bytes 786464 | tf_op jit(solution)/shard_map/ppermute | solution.py:13
  230.3 2.0 collective-permute-start.38
  233.8 39.1 %collective-permute-done.24 = bf16[192,2048]{1,0:T(8,128)(2,1)S(1)} collective-permute-done((bf16[192,2048]{1,0:T(8,128)(2,1)S(1)}, bf16[192,2048]{1,0:T(8,128)(2,1)S(1)}, u32[]{:S(2)}, u32[]{:S(2)}) %collective-permute-start.24) | collective-permute-done | bytes 786464 | tf_op jit(solution)/shard_map/ppermute | solution.py:13
  272.9 3.9 collective-permute-start.22
  277.6 14.2 %collective-permute-done.22 = bf16[192,2048]{1,0:T(8,128)(2,1)S(1)} collective-permute-done((bf16[192,2048]{1,0:T(8,128)(2,1)S(1)}, bf16[192,2048]{1,0:T(8,128)(2,1)S(1)}, u32[]{:S(2)}, u32[]{:S(2)}) %collective-permute-start.22) | collective-permute-done | bytes 786464 | tf_op jit(solution)/shard_map/ppermute | solution.py:13
  294.4 1.8 collective-permute-start.36
  298.1 8.2 %multiply_convert_fusion = (bf16[384,2048]{1,0:T(8,128)(2,1)}, bf16[384,2048]{1,0:T(8,128)(2,1)}) fusion(bf16[192,2048]{1,0:T(8,128)(2,1)} %copy-done.24, bf16[192,2048]{1,0:T(8,128)(2,1)} %copy-done.25, bf16[192,2048]{1,0:T(8,128)(2,1)S(1)} %collective-permute-done.24, bf16[192,2048]{1,0:T(8,128)(2,1)} %copy-done.23, bf16[384,2048]{1,0:T(8,128)(2,1)} %copy-done.21, ...), kind=kOutput, calls=%fused_computation.31 | convolution fusion | flops 1636564992 | bytes 23855104 | tf_op jit(solution)/shard_map/dot_general | solution.py:53
  307.5 5.8 %collective-permute-done.35 = bf16[192,2048]{1,0:T(8,128)(2,1)S(1)} collective-permute-done((bf16[192,2048]{1,0:T(8,128)(2,1)S(1)}, bf16[192,2048]{1,0:T(8,128)(2,1)S(1)}, u32[]{:S(2)}, u32[]{:S(2)}) %collective-permute-start.35) | collective-permute-done | bytes 786464 | tf_op jit(solution)/shard_map/ppermute | solution.py:13
  315.1 3.5 fusion.110
  318.6 3.2 add_convert_fusion.6
  322.4 1.8 collective-permute-start.46
  325.8 8.3 %collective-permute-start.40 = (bf16[1,384,128]{2,1,0:T(8,128)(2,1)S(1)}, bf16[1,384,128]{2,1,0:T(8,128)(2,1)S(1)}, u32[]{:S(2)}, u32[]{:S(2)}) collective-permute-start(bf16[1,384,128]{2,1,0:T(8,128)(2,1)S(1)} %get-tuple-element.99), channel_id=1, source_target_pairs={{0,2},{1,3},{2,4},{3,5},{4,6},{5,7},{6,0},{7,1},{8,10},{9,11},{10,... | collective-permute-start | bytes 294920 | tf_op jit(solution)/shard_map/ppermute | solution.py:30
  334.1 14.5 %collective-permute-done.44 = bf16[384,2048]{1,0:T(8,128)(2,1)S(1)} collective-permute-done((bf16[384,2048]{1,0:T(8,128)(2,1)}, bf16[384,2048]{1,0:T(8,128)(2,1)S(1)}, u32[]{:S(2)}, u32[]{:S(2)}) %collective-permute-start.44) | collective-permute-done | bytes 1572896 | tf_op jit(solution)/shard_map/ppermute | solution.py:13
  348.6 11.8 %collective-permute-start.42 = (bf16[1,384,128]{2,1,0:T(8,128)(2,1)S(1)}, bf16[1,384,128]{2,1,0:T(8,128)(2,1)S(1)}, u32[]{:S(2)}, u32[]{:S(2)}) collective-permute-start(bf16[1,384,128]{2,1,0:T(8,128)(2,1)S(1)} %get-tuple-element.97), channel_id=1, source_target_pairs={{0,6},{1,7},{2,0},{3,1},{4,2},{5,3},{6,4},{7,5},{8,14},{9,15},{10,... | collective-permute-start | bytes 294920 | tf_op jit(solution)/shard_map/ppermute | solution.py:30
  360.4 1.8 fusion.112
  363.3 1.8 fusion.111
  365.2 14.4 %collective-permute-done.46 = bf16[384,2048]{1,0:T(8,128)(2,1)S(1)} collective-permute-done((bf16[384,2048]{1,0:T(8,128)(2,1)}, bf16[384,2048]{1,0:T(8,128)(2,1)S(1)}, u32[]{:S(2)}, u32[]{:S(2)}) %collective-permute-start.46) | collective-permute-done | bytes 1572896 | tf_op jit(solution)/shard_map/ppermute | solution.py:13
  381.4 1.8 fusion.114
  384.6 1.8 fusion.113
  388.4 8.5 %fusion.24 = bf16[2048,1024]{1,0:T(8,128)(2,1)} fusion(bf16[1536,1024]{1,0:T(8,128)(2,1)S(1)} %pad_maximum_fusion.1, bf16[384,2048]{1,0:T(8,128)(2,1)S(1)} %pad_maximum_fusion.3, bf16[384,2048]{1,0:T(8,128)(2,1)S(1)} %copy-done.8, bf16[384,2048]{1,0:T(8,128)(2,1)S(1)} %collective-permute-done.33, bf16[384,2048]{1,0:T(8,128)(2,1)S(1)} %copy-done.20), kind=kOutput, calls=%fused_computation.26 | convolution fusion | flops 6469713920 | bytes 13631488 | tf_op jit(solution)/shard_map/dot_general | solution.py:59
  397.6 7.3 %collective-permute-start.41 = (bf16[1,384,128]{2,1,0:T(8,128)(2,1)S(1)}, bf16[1,384,128]{2,1,0:T(8,128)(2,1)S(1)}, u32[]{:S(2)}, u32[]{:S(2)}) collective-permute-start(bf16[1,384,128]{2,1,0:T(8,128)(2,1)S(1)} %get-tuple-element.98), channel_id=1, source_target_pairs={{0,4},{1,5},{2,6},{3,7},{4,0},{5,1},{6,2},{7,3},{8,12},{9,13},{10,... | collective-permute-start | bytes 294920 | tf_op jit(solution)/shard_map/ppermute | solution.py:30
  405.1 5.9 %collective-permute-done.53 = bf16[192,2048]{1,0:T(8,128)(2,1)S(1)} collective-permute-done((bf16[192,2048]{1,0:T(8,128)(2,1)S(1)}, bf16[192,2048]{1,0:T(8,128)(2,1)S(1)}, u32[]{:S(2)}, u32[]{:S(2)}) %collective-permute-start.53) | collective-permute-done | bytes 786464 | tf_op jit(solution)/shard_map/ppermute | solution.py:13
  413.3 7.7 %collective-permute-start.49 = (bf16[2,384,128]{2,1,0:T(8,128)(2,1)S(1)}, bf16[2,384,128]{2,1,0:T(8,128)(2,1)S(1)}, u32[]{:S(2)}, u32[]{:S(2)}) collective-permute-start(bf16[2,384,128]{2,1,0:T(8,128)(2,1)S(1)} %get-tuple-element.89), channel_id=1, source_target_pairs={{0,4},{1,5},{2,6},{3,7},{4,0},{5,1},{6,2},{7,3},{8,12},{9,13},{10,... | collective-permute-start | bytes 589832 | tf_op jit(solution)/shard_map/ppermute | solution.py:30
  421.0 5.0 %collective-permute-start.48 = (bf16[2,384,128]{2,1,0:T(8,128)(2,1)S(1)}, bf16[2,384,128]{2,1,0:T(8,128)(2,1)S(1)}, u32[]{:S(2)}, u32[]{:S(2)}) collective-permute-start(bf16[2,384,128]{2,1,0:T(8,128)(2,1)S(1)} %get-tuple-element.90), channel_id=1, source_target_pairs={{0,2},{1,3},{2,4},{3,5},{4,6},{5,7},{6,0},{7,1},{8,10},{9,11},{10,... | collective-permute-start | bytes 589832 | tf_op jit(solution)/shard_map/ppermute | solution.py:30
  426.2 1.8 fusion.115
  428.1 1.8 add_convert_fusion.2
  430.1 3.0 collective-permute-done.48
  433.1 2.1 collective-permute-done.50
  435.5 4.3 collective-permute-start.57
  439.8 3.8 collective-permute-start.58
  443.7 2.6 collective-permute-done.56
  448.0 3.2 fusion.40
  451.2 4.2 all-to-all-start
  455.4 10.2 %fusion.27 = bf16[1024,2048]{1,0:T(8,128)(2,1)} fusion(bf16[1536,1024]{1,0:T(8,128)(2,1)S(1)} %pad_maximum_fusion, bf16[384,2048]{1,0:T(8,128)(2,1)} %copy-done.2, bf16[384,2048]{1,0:T(8,128)(2,1)} %copy-done.3, bf16[384,2048]{1,0:T(8,128)(2,1)} %copy-done.5, bf16[384,2048]{1,0:T(8,128)(2,1)} %get-tuple-element.53), kind=kOutput, calls=%fused_computation.27 | convolution fusion | flops 6469713920 | bytes 13631488 | tf_op jit(solution)/shard_map/dot_general | solution.py:59
  466.7 3.7 collective-permute-start.59
  471.1 10.2 %fusion.30 = bf16[1024,2048]{1,0:T(8,128)(2,1)} fusion(bf16[1536,1024]{1,0:T(8,128)(2,1)S(1)} %pad_maximum_fusion, bf16[384,2048]{1,0:T(8,128)(2,1)} %copy-done.1, bf16[384,2048]{1,0:T(8,128)(2,1)} %copy-done.4, bf16[384,2048]{1,0:T(8,128)(2,1)} %copy-done.6, bf16[384,2048]{1,0:T(8,128)(2,1)} %get-tuple-element.54), kind=kOutput, calls=%fused_computation.28 | convolution fusion | flops 6469713920 | bytes 13631488 | tf_op jit(solution)/shard_map/dot_general | solution.py:59
  (232 shorter events, 66.0 us)
Async XLA Ops:
  0.6 11.4 %collective-permute-start = (s32[1,4]{1,0:T(1,128)}, s32[1,4]{1,0:T(1,128)S(1)}, u32[]{:S(2)}, u32[]{:S(2)}) collective-permute-start(s32[1,4]{1,0:T(1,128)} %param.8), channel_id=1, source_target_pairs={{0,8},{8,0},{16,24},{24,16},{1,9},{9,1},{17,25},{25,17},{2,10},{10... | collective-permute-start | bytes 56 | tf_op jit(solution)/shard_map/ppermute | solution.py:13
  3.7 12.0 %collective-permute-start.1 = (s32[1,4]{1,0:T(1,128)}, s32[1,4]{1,0:T(1,128)S(1)}, u32[]{:S(2)}, u32[]{:S(2)}) collective-permute-start(s32[1,4]{1,0:T(1,128)} %param.8), channel_id=1, source_target_pairs={{0,16},{8,24},{16,0},{24,8},{1,17},{9,25},{17,1},{25,9},{2,18},{10... | collective-permute-start | bytes 56 | tf_op jit(solution)/shard_map/ppermute | solution.py:13
  5.2 12.8 %collective-permute-start.2 = (s32[1,4]{1,0:T(1,128)}, s32[1,4]{1,0:T(1,128)S(1)}, u32[]{:S(2)}, u32[]{:S(2)}) collective-permute-start(s32[1,4]{1,0:T(1,128)} %param.8), channel_id=1, source_target_pairs={{0,24},{8,16},{16,8},{24,0},{1,25},{9,17},{17,9},{25,1},{2,26},{10... | collective-permute-start | bytes 56 | tf_op jit(solution)/shard_map/ppermute | solution.py:13
  6.3 13.6 %collective-permute-start.3 = (bf16[96,512]{1,0:T(8,128)(2,1)S(1)}, bf16[96,512]{1,0:T(8,128)(2,1)S(1)}, u32[]{:S(2)}, u32[]{:S(2)}) collective-permute-start(bf16[96,512]{1,0:T(8,128)(2,1)S(1)} %get-tuple-element.122), channel_id=1, source_target_pairs={{0,0},{1,1},{2,8},{3,9},{4,16},{5,17},{6,24},{7,25},{8,2},{9,3},{1... | collective-permute-start | bytes 294920 | tf_op jit(solution)/shard_map/ppermute | solution.py:45
  7.0 12.9 %collective-permute-start.4 = (bf16[96,512]{1,0:T(8,128)(2,1)S(1)}, bf16[96,512]{1,0:T(8,128)(2,1)S(1)}, u32[]{:S(2)}, u32[]{:S(2)}) collective-permute-start(bf16[96,512]{1,0:T(8,128)(2,1)S(1)} %get-tuple-element.121), channel_id=1, source_target_pairs={{0,2},{1,3},{2,10},{3,11},{4,18},{5,19},{6,26},{7,27},{8,4},{9,5},... | collective-permute-start | bytes 294920 | tf_op jit(solution)/shard_map/ppermute | solution.py:45
  12.1 7.8 %collective-permute-start.5 = (bf16[96,512]{1,0:T(8,128)(2,1)S(1)}, bf16[96,512]{1,0:T(8,128)(2,1)S(1)}, u32[]{:S(2)}, u32[]{:S(2)}) collective-permute-start(bf16[96,512]{1,0:T(8,128)(2,1)S(1)} %get-tuple-element.120), channel_id=1, source_target_pairs={{0,4},{1,5},{2,12},{3,13},{4,20},{5,21},{6,28},{7,29},{8,6},{9,7},... | collective-permute-start | bytes 294920 | tf_op jit(solution)/shard_map/ppermute | solution.py:45
  15.6 6.0 %collective-permute-start.6 = (bf16[96,512]{1,0:T(8,128)(2,1)S(1)}, bf16[96,512]{1,0:T(8,128)(2,1)S(1)}, u32[]{:S(2)}, u32[]{:S(2)}) collective-permute-start(bf16[96,512]{1,0:T(8,128)(2,1)S(1)} %get-tuple-element.119), channel_id=1, source_target_pairs={{0,6},{1,7},{2,14},{3,15},{4,22},{5,23},{6,30},{7,31},{8,0},{9,1},... | collective-permute-start | bytes 294920 | tf_op jit(solution)/shard_map/ppermute | solution.py:45
  21.7 12.8 %collective-permute-start.7 = (bf16[96,512]{1,0:T(8,128)(2,1)S(1)}, bf16[96,512]{1,0:T(8,128)(2,1)S(1)}, u32[]{:S(2)}, u32[]{:S(2)}) collective-permute-start(bf16[96,512]{1,0:T(8,128)(2,1)S(1)} %get-tuple-element.115), channel_id=1, source_target_pairs={{0,0},{1,1},{2,8},{3,9},{4,16},{5,17},{6,24},{7,25},{8,2},{9,3},{1... | collective-permute-start | bytes 294920 | tf_op jit(solution)/shard_map/ppermute | solution.py:45
  22.4 12.4 %collective-permute-start.8 = (bf16[96,512]{1,0:T(8,128)(2,1)S(1)}, bf16[96,512]{1,0:T(8,128)(2,1)S(1)}, u32[]{:S(2)}, u32[]{:S(2)}) collective-permute-start(bf16[96,512]{1,0:T(8,128)(2,1)S(1)} %get-tuple-element.118), channel_id=1, source_target_pairs={{0,2},{1,3},{2,10},{3,11},{4,18},{5,19},{6,26},{7,27},{8,4},{9,5},... | collective-permute-start | bytes 294920 | tf_op jit(solution)/shard_map/ppermute | solution.py:45
  28.7 8.8 %collective-permute-start.9 = (bf16[96,512]{1,0:T(8,128)(2,1)S(1)}, bf16[96,512]{1,0:T(8,128)(2,1)S(1)}, u32[]{:S(2)}, u32[]{:S(2)}) collective-permute-start(bf16[96,512]{1,0:T(8,128)(2,1)S(1)} %get-tuple-element.117), channel_id=1, source_target_pairs={{0,4},{1,5},{2,12},{3,13},{4,20},{5,21},{6,28},{7,29},{8,6},{9,7},... | collective-permute-start | bytes 294920 | tf_op jit(solution)/shard_map/ppermute | solution.py:45
  30.2 8.4 %collective-permute-start.10 = (bf16[96,512]{1,0:T(8,128)(2,1)S(1)}, bf16[96,512]{1,0:T(8,128)(2,1)S(1)}, u32[]{:S(2)}, u32[]{:S(2)}) collective-permute-start(bf16[96,512]{1,0:T(8,128)(2,1)S(1)} %get-tuple-element.116), channel_id=1, source_target_pairs={{0,6},{1,7},{2,14},{3,15},{4,22},{5,23},{6,30},{7,31},{8,0},{9,1},... | collective-permute-start | bytes 294920 | tf_op jit(solution)/shard_map/ppermute | solution.py:45
  32.8 9.2 %collective-permute-start.25 = (bf16[1,96,512]{2,1,0:T(8,128)(2,1)S(1)}, bf16[1,96,512]{2,1,0:T(8,128)(2,1)S(1)}, u32[]{:S(2)}, u32[]{:S(2)}) collective-permute-start(bf16[1,96,512]{2,1,0:T(8,128)(2,1)S(1)} %get-tuple-element.105), channel_id=1, source_target_pairs={{0,2},{1,3},{2,4},{3,5},{4,6},{5,7},{6,0},{7,1},{8,10},{9,11},{10,... | collective-permute-start | bytes 294920 | tf_op jit(solution)/shard_map/ppermute | solution.py:30
  34.5 20.6 %collective-permute-start.26 = (bf16[1,96,512]{2,1,0:T(8,128)(2,1)S(1)}, bf16[1,96,512]{2,1,0:T(8,128)(2,1)S(1)}, u32[]{:S(2)}, u32[]{:S(2)}) collective-permute-start(bf16[1,96,512]{2,1,0:T(8,128)(2,1)S(1)} %get-tuple-element.105), channel_id=1, source_target_pairs={{0,4},{1,5},{2,6},{3,7},{4,0},{5,1},{6,2},{7,3},{8,12},{9,13},{10,... | collective-permute-start | bytes 294920 | tf_op jit(solution)/shard_map/ppermute | solution.py:30
  34.8 20.4 %collective-permute-start.27 = (bf16[1,96,512]{2,1,0:T(8,128)(2,1)S(1)}, bf16[1,96,512]{2,1,0:T(8,128)(2,1)S(1)}, u32[]{:S(2)}, u32[]{:S(2)}) collective-permute-start(bf16[1,96,512]{2,1,0:T(8,128)(2,1)S(1)} %get-tuple-element.105), channel_id=1, source_target_pairs={{0,6},{1,7},{2,0},{3,1},{4,2},{5,3},{6,4},{7,5},{8,14},{9,15},{10,... | collective-permute-start | bytes 294920 | tf_op jit(solution)/shard_map/ppermute | solution.py:30
  37.5 20.5 %collective-permute-start.15 = (bf16[3,96,512]{2,1,0:T(8,128)(2,1)}, bf16[3,96,512]{2,1,0:T(8,128)(2,1)S(1)}, u32[]{:S(2)}, u32[]{:S(2)}) collective-permute-start(bf16[3,96,512]{2,1,0:T(8,128)(2,1)} %get-tuple-element.124), channel_id=1, source_target_pairs={{0,2},{1,3},{2,4},{3,5},{4,6},{5,7},{6,0},{7,1},{8,10},{9,11},{10,... | collective-permute-start | bytes 884744 | tf_op jit(solution)/shard_map/ppermute | solution.py:30
  38.6 43.0 %collective-permute-start.16 = (bf16[3,96,512]{2,1,0:T(8,128)(2,1)}, bf16[3,96,512]{2,1,0:T(8,128)(2,1)S(1)}, u32[]{:S(2)}, u32[]{:S(2)}) collective-permute-start(bf16[3,96,512]{2,1,0:T(8,128)(2,1)} %get-tuple-element.124), channel_id=1, source_target_pairs={{0,4},{1,5},{2,6},{3,7},{4,0},{5,1},{6,2},{7,3},{8,12},{9,13},{10,... | collective-permute-start | bytes 884744 | tf_op jit(solution)/shard_map/ppermute | solution.py:30
  42.0 41.0 %collective-permute-start.17 = (bf16[3,96,512]{2,1,0:T(8,128)(2,1)}, bf16[3,96,512]{2,1,0:T(8,128)(2,1)}, u32[]{:S(2)}, u32[]{:S(2)}) collective-permute-start(bf16[3,96,512]{2,1,0:T(8,128)(2,1)} %get-tuple-element.124), channel_id=1, source_target_pairs={{0,6},{1,7},{2,0},{3,1},{4,2},{5,3},{6,4},{7,5},{8,14},{9,15},{10,... | collective-permute-start | bytes 884744 | tf_op jit(solution)/shard_map/ppermute | solution.py:30
  55.1 29.2 %collective-permute-start.11 = (bf16[4,96,512]{2,1,0:T(8,128)(2,1)S(1)}, bf16[4,96,512]{2,1,0:T(8,128)(2,1)S(1)}, u32[]{:S(2)}, u32[]{:S(2)}) collective-permute-start(bf16[4,96,512]{2,1,0:T(8,128)(2,1)S(1)} %get-tuple-element.110), channel_id=1, source_target_pairs={{0,2},{1,3},{2,4},{3,5},{4,6},{5,7},{6,0},{7,1},{8,10},{9,11},{10,... | collective-permute-start | bytes 1179656 | tf_op jit(solution)/shard_map/ppermute | solution.py:30
  55.1 41.2 %collective-permute-start.12 = (bf16[4,96,512]{2,1,0:T(8,128)(2,1)S(1)}, bf16[4,96,512]{2,1,0:T(8,128)(2,1)S(1)}, u32[]{:S(2)}, u32[]{:S(2)}) collective-permute-start(bf16[4,96,512]{2,1,0:T(8,128)(2,1)S(1)} %get-tuple-element.110), channel_id=1, source_target_pairs={{0,4},{1,5},{2,6},{3,7},{4,0},{5,1},{6,2},{7,3},{8,12},{9,13},{10,... | collective-permute-start | bytes 1179656 | tf_op jit(solution)/shard_map/ppermute | solution.py:30
  58.0 38.4 %collective-permute-start.13 = (bf16[4,96,512]{2,1,0:T(8,128)(2,1)S(1)}, bf16[4,96,512]{2,1,0:T(8,128)(2,1)S(1)}, u32[]{:S(2)}, u32[]{:S(2)}) collective-permute-start(bf16[4,96,512]{2,1,0:T(8,128)(2,1)S(1)} %get-tuple-element.110), channel_id=1, source_target_pairs={{0,6},{1,7},{2,0},{3,1},{4,2},{5,3},{6,4},{7,5},{8,14},{9,15},{10,... | collective-permute-start | bytes 1179656 | tf_op jit(solution)/shard_map/ppermute | solution.py:30
  81.6 15.0 %collective-permute-start.28 = (bf16[1,4,96,512]{3,2,0,1:T(8,128)(2,1)S(1)}, bf16[1,4,96,512]{3,2,0,1:T(8,128)(2,1)S(1)}, u32[]{:S(2)}, u32[]{:S(2)}) collective-permute-start(bf16[1,4,96,512]{3,2,0,1:T(8,128)(2,1)S(1)} %pad_maximum_fusion.19), channel_id=1, source_target_pairs={{0,1},{1,0},{2,3},{3,2},{4,5},{5,4},{6,7},{7,6},{8,9},{9,8},{10,11... | collective-permute-start | bytes 1179656 | tf_op jit(solution)/shard_map/ppermute | solution.py:35
  84.3 22.6 %collective-permute-start.18 = (bf16[3,4,96,512]{3,2,0,1:T(8,128)(2,1)S(1)}, bf16[3,4,96,512]{3,2,0,1:T(8,128)(2,1)S(1)}, u32[]{:S(2)}, u32[]{:S(2)}) collective-permute-start(bf16[3,4,96,512]{3,2,0,1:T(8,128)(2,1)S(1)} %pad_maximum_fusion.6), channel_id=1, source_target_pairs={{0,1},{1,0},{2,3},{3,2},{4,5},{5,4},{6,7},{7,6},{8,9},{9,8},{10,11... | collective-permute-start | bytes 3538952 | tf_op jit(solution)/shard_map/ppermute | solution.py:35
  96.5 49.2 %collective-permute-start.14 = (bf16[4,4,96,512]{3,2,0,1:T(8,128)(2,1)S(1)}, bf16[4,4,96,512]{3,2,0,1:T(8,128)(2,1)S(1)}, u32[]{:S(2)}, u32[]{:S(2)}) collective-permute-start(bf16[4,4,96,512]{3,2,0,1:T(8,128)(2,1)S(1)} %pad_maximum_fusion.2), channel_id=1, source_target_pairs={{0,1},{1,0},{2,3},{3,2},{4,5},{5,4},{6,7},{7,6},{8,9},{9,8},{10,11... | collective-permute-start | bytes 4718600 | tf_op jit(solution)/shard_map/ppermute | solution.py:35
  100.3 37.7 %collective-permute-start.29 = (bf16[384,2048]{1,0:T(8,128)(2,1)S(1)}, bf16[384,2048]{1,0:T(8,128)(2,1)S(1)}, u32[]{:S(2)}, u32[]{:S(2)}) collective-permute-start(bf16[384,2048]{1,0:T(8,128)(2,1)S(1)} %convolution_convert_fusion.1), channel_id=1, source_target_pairs={{0,8},{8,0},{16,24},{24,16},{1,9},{9,1},{17,25},{25,17},{2,10},{10... | collective-permute-start | bytes 4718600 | tf_op jit(solution)/shard_map/ppermute | solution.py:13
  104.6 39.3 %collective-permute-start.31 = (bf16[384,2048]{1,0:T(8,128)(2,1)S(1)}, bf16[384,2048]{1,0:T(8,128)(2,1)S(1)}, u32[]{:S(2)}, u32[]{:S(2)}) collective-permute-start(bf16[384,2048]{1,0:T(8,128)(2,1)S(1)} %convolution_convert_fusion), channel_id=1, source_target_pairs={{0,16},{8,24},{16,0},{24,8},{1,17},{9,25},{17,1},{25,9},{2,18},{10... | collective-permute-start | bytes 4718600 | tf_op jit(solution)/shard_map/ppermute | solution.py:13
  108.9 67.0 %collective-permute-start.20 = (bf16[384,2048]{1,0:T(8,128)(2,1)S(1)}, bf16[384,2048]{1,0:T(8,128)(2,1)S(1)}, u32[]{:S(2)}, u32[]{:S(2)}) collective-permute-start(bf16[384,2048]{1,0:T(8,128)(2,1)S(1)} %convolution_convert_fusion.2), channel_id=1, source_target_pairs={{0,16},{8,24},{16,0},{24,8},{1,17},{9,25},{17,1},{25,9},{2,18},{10... | collective-permute-start | bytes 4718600 | tf_op jit(solution)/shard_map/ppermute | solution.py:13
  110.8 65.1 %collective-permute-start.19 = (bf16[384,2048]{1,0:T(8,128)(2,1)S(1)}, bf16[384,2048]{1,0:T(8,128)(2,1)S(1)}, u32[]{:S(2)}, u32[]{:S(2)}) collective-permute-start(bf16[384,2048]{1,0:T(8,128)(2,1)S(1)} %convolution_convert_fusion.3), channel_id=1, source_target_pairs={{0,8},{8,0},{16,24},{24,16},{1,9},{9,1},{17,25},{25,17},{2,10},{10... | collective-permute-start | bytes 4718600 | tf_op jit(solution)/shard_map/ppermute | solution.py:13
  114.3 95.3 %copy-start.26 = (f32[384,2048]{1,0:T(8,128)}, f32[384,2048]{1,0:T(8,128)S(1)}, u32[]{:S(2)}) copy-start(f32[384,2048]{1,0:T(8,128)S(1)} %fusion.104) | copy-start | bytes 9437188
  139.9 69.7 %collective-permute-start.30 = (bf16[384,2048]{1,0:T(8,128)(2,1)S(1)}, bf16[384,2048]{1,0:T(8,128)(2,1)S(1)}, u32[]{:S(2)}, u32[]{:S(2)}) collective-permute-start(bf16[384,2048]{1,0:T(8,128)(2,1)S(1)} %add_convert_fusion.1), channel_id=1, source_target_pairs={{0,16},{8,24},{16,0},{24,8},{1,17},{9,25},{17,1},{25,9},{2,18},{10... | collective-permute-start | bytes 4718600 | tf_op jit(solution)/shard_map/ppermute | solution.py:13
  145.7 63.9 %collective-permute-start.32 = (bf16[384,2048]{1,0:T(8,128)(2,1)S(1)}, bf16[384,2048]{1,0:T(8,128)(2,1)S(1)}, u32[]{:S(2)}, u32[]{:S(2)}) collective-permute-start(bf16[384,2048]{1,0:T(8,128)(2,1)S(1)} %add_convert_fusion), channel_id=1, source_target_pairs={{0,8},{8,0},{16,24},{24,16},{1,9},{9,1},{17,25},{25,17},{2,10},{10... | collective-permute-start | bytes 4718600 | tf_op jit(solution)/shard_map/ppermute | solution.py:13
  175.9 50.6 %collective-permute-start.23 = (bf16[192,2048]{1,0:T(8,128)(2,1)S(1)}, bf16[192,2048]{1,0:T(8,128)(2,1)S(1)}, u32[]{:S(2)}, u32[]{:S(2)}) collective-permute-start(bf16[192,2048]{1,0:T(8,128)(2,1)S(1)} %convolution_convert_fusion.6), channel_id=1, source_target_pairs={{0,16},{8,24},{16,0},{24,8},{1,17},{9,25},{17,1},{25,9},{2,18},{10... | collective-permute-start | bytes 2359304 | tf_op jit(solution)/shard_map/ppermute | solution.py:13
  177.9 52.4 %collective-permute-start.21 = (bf16[192,2048]{1,0:T(8,128)(2,1)S(1)}, bf16[192,2048]{1,0:T(8,128)(2,1)S(1)}, u32[]{:S(2)}, u32[]{:S(2)}) collective-permute-start(bf16[192,2048]{1,0:T(8,128)(2,1)S(1)} %convolution_convert_fusion.7), channel_id=1, source_target_pairs={{0,8},{8,0},{16,24},{24,16},{1,9},{9,1},{17,25},{25,17},{2,10},{10... | collective-permute-start | bytes 2359304 | tf_op jit(solution)/shard_map/ppermute | solution.py:13
  213.9 77.9 %collective-permute-start.33 = (bf16[384,2048]{1,0:T(8,128)(2,1)S(1)}, bf16[384,2048]{1,0:T(8,128)(2,1)S(1)}, u32[]{:S(2)}, u32[]{:S(2)}) collective-permute-start(bf16[384,2048]{1,0:T(8,128)(2,1)S(1)} %get-tuple-element.133), channel_id=1, source_target_pairs={{0,8},{8,0},{16,24},{24,16},{1,9},{9,1},{17,25},{25,17},{2,10},{10... | collective-permute-start | bytes 4718600 | tf_op jit(solution)/shard_map/ppermute | solution.py:13
  215.7 77.1 %collective-permute-start.34 = (bf16[384,2048]{1,0:T(8,128)(2,1)S(1)}, bf16[384,2048]{1,0:T(8,128)(2,1)S(1)}, u32[]{:S(2)}, u32[]{:S(2)}) collective-permute-start(bf16[384,2048]{1,0:T(8,128)(2,1)S(1)} %get-tuple-element.133), channel_id=1, source_target_pairs={{0,16},{8,24},{16,0},{24,8},{1,17},{9,25},{17,1},{25,9},{2,18},{10... | collective-permute-start | bytes 4718600 | tf_op jit(solution)/shard_map/ppermute | solution.py:13
  228.0 44.9 %collective-permute-start.24 = (bf16[192,2048]{1,0:T(8,128)(2,1)S(1)}, bf16[192,2048]{1,0:T(8,128)(2,1)S(1)}, u32[]{:S(2)}, u32[]{:S(2)}) collective-permute-start(bf16[192,2048]{1,0:T(8,128)(2,1)S(1)} %add_convert_fusion.7), channel_id=1, source_target_pairs={{0,8},{8,0},{16,24},{24,16},{1,9},{9,1},{17,25},{25,17},{2,10},{10... | collective-permute-start | bytes 2359304 | tf_op jit(solution)/shard_map/ppermute | solution.py:13
  229.9 66.4 %collective-permute-start.37 = (bf16[192,2048]{1,0:T(8,128)(2,1)S(1)}, bf16[192,2048]{1,0:T(8,128)(2,1)S(1)}, u32[]{:S(2)}, u32[]{:S(2)}) collective-permute-start(bf16[192,2048]{1,0:T(8,128)(2,1)S(1)} %convolution_convert_fusion.5), channel_id=1, source_target_pairs={{0,8},{8,0},{16,24},{24,16},{1,9},{9,1},{17,25},{25,17},{2,10},{10... | collective-permute-start | bytes 2359304 | tf_op jit(solution)/shard_map/ppermute | solution.py:13
  230.3 66.0 %collective-permute-start.38 = (bf16[192,2048]{1,0:T(8,128)(2,1)S(1)}, bf16[192,2048]{1,0:T(8,128)(2,1)S(1)}, u32[]{:S(2)}, u32[]{:S(2)}) collective-permute-start(bf16[192,2048]{1,0:T(8,128)(2,1)S(1)} %convolution_convert_fusion.4), channel_id=1, source_target_pairs={{0,16},{8,24},{16,0},{24,8},{1,17},{9,25},{17,1},{25,9},{2,18},{10... | collective-permute-start | bytes 2359304 | tf_op jit(solution)/shard_map/ppermute | solution.py:13
  272.9 18.9 %collective-permute-start.22 = (bf16[192,2048]{1,0:T(8,128)(2,1)S(1)}, bf16[192,2048]{1,0:T(8,128)(2,1)S(1)}, u32[]{:S(2)}, u32[]{:S(2)}) collective-permute-start(bf16[192,2048]{1,0:T(8,128)(2,1)S(1)} %add_convert_fusion.8), channel_id=1, source_target_pairs={{0,16},{8,24},{16,0},{24,8},{1,17},{9,25},{17,1},{25,9},{2,18},{10... | collective-permute-start | bytes 2359304 | tf_op jit(solution)/shard_map/ppermute | solution.py:13
  292.9 20.5 %collective-permute-start.35 = (bf16[192,2048]{1,0:T(8,128)(2,1)S(1)}, bf16[192,2048]{1,0:T(8,128)(2,1)S(1)}, u32[]{:S(2)}, u32[]{:S(2)}) collective-permute-start(bf16[192,2048]{1,0:T(8,128)(2,1)S(1)} %slice.176), channel_id=1, source_target_pairs={{0,8},{8,0},{16,24},{24,16},{1,9},{9,1},{17,25},{25,17},{2,10},{10... | collective-permute-start | bytes 2359304 | tf_op jit(solution)/shard_map/ppermute | solution.py:13
  294.4 20.5 %collective-permute-start.36 = (bf16[192,2048]{1,0:T(8,128)(2,1)S(1)}, bf16[192,2048]{1,0:T(8,128)(2,1)S(1)}, u32[]{:S(2)}, u32[]{:S(2)}) collective-permute-start(bf16[192,2048]{1,0:T(8,128)(2,1)S(1)} %slice.177), channel_id=1, source_target_pairs={{0,16},{8,24},{16,0},{24,8},{1,17},{9,25},{17,1},{25,9},{2,18},{10... | collective-permute-start | bytes 2359304 | tf_op jit(solution)/shard_map/ppermute | solution.py:13
  306.3 42.3 %collective-permute-start.44 = (bf16[384,2048]{1,0:T(8,128)(2,1)}, bf16[384,2048]{1,0:T(8,128)(2,1)S(1)}, u32[]{:S(2)}, u32[]{:S(2)}) collective-permute-start(bf16[384,2048]{1,0:T(8,128)(2,1)} %get-tuple-element.53), channel_id=1, source_target_pairs={{0,16},{8,24},{16,0},{24,8},{1,17},{9,25},{17,1},{25,9},{2,18},{10... | collective-permute-start | bytes 4718600 | tf_op jit(solution)/shard_map/ppermute | solution.py:13
  306.6 55.7 %collective-permute-start.43 = (bf16[384,2048]{1,0:T(8,128)(2,1)}, bf16[384,2048]{1,0:T(8,128)(2,1)S(1)}, u32[]{:S(2)}, u32[]{:S(2)}) collective-permute-start(bf16[384,2048]{1,0:T(8,128)(2,1)} %get-tuple-element.53), channel_id=1, source_target_pairs={{0,8},{8,0},{16,24},{24,16},{1,9},{9,1},{17,25},{25,17},{2,10},{10... | collective-permute-start | bytes 4718600 | tf_op jit(solution)/shard_map/ppermute | solution.py:13
  321.9 3.6 collective-permute-start.39
  322.4 57.2 %collective-permute-start.46 = (bf16[384,2048]{1,0:T(8,128)(2,1)}, bf16[384,2048]{1,0:T(8,128)(2,1)S(1)}, u32[]{:S(2)}, u32[]{:S(2)}) collective-permute-start(bf16[384,2048]{1,0:T(8,128)(2,1)} %get-tuple-element.54), channel_id=1, source_target_pairs={{0,16},{8,24},{16,0},{24,8},{1,17},{9,25},{17,1},{25,9},{2,18},{10... | collective-permute-start | bytes 4718600 | tf_op jit(solution)/shard_map/ppermute | solution.py:13
  324.6 59.0 %collective-permute-start.45 = (bf16[384,2048]{1,0:T(8,128)(2,1)}, bf16[384,2048]{1,0:T(8,128)(2,1)S(1)}, u32[]{:S(2)}, u32[]{:S(2)}) collective-permute-start(bf16[384,2048]{1,0:T(8,128)(2,1)} %get-tuple-element.54), channel_id=1, source_target_pairs={{0,8},{8,0},{16,24},{24,16},{1,9},{9,1},{17,25},{25,17},{2,10},{10... | collective-permute-start | bytes 4718600 | tf_op jit(solution)/shard_map/ppermute | solution.py:13
  325.8 61.2 %collective-permute-start.40 = (bf16[1,384,128]{2,1,0:T(8,128)(2,1)S(1)}, bf16[1,384,128]{2,1,0:T(8,128)(2,1)S(1)}, u32[]{:S(2)}, u32[]{:S(2)}) collective-permute-start(bf16[1,384,128]{2,1,0:T(8,128)(2,1)S(1)} %get-tuple-element.99), channel_id=1, source_target_pairs={{0,2},{1,3},{2,4},{3,5},{4,6},{5,7},{6,0},{7,1},{8,10},{9,11},{10,... | collective-permute-start | bytes 294920 | tf_op jit(solution)/shard_map/ppermute | solution.py:30
  348.6 38.7 %collective-permute-start.42 = (bf16[1,384,128]{2,1,0:T(8,128)(2,1)S(1)}, bf16[1,384,128]{2,1,0:T(8,128)(2,1)S(1)}, u32[]{:S(2)}, u32[]{:S(2)}) collective-permute-start(bf16[1,384,128]{2,1,0:T(8,128)(2,1)S(1)} %get-tuple-element.97), channel_id=1, source_target_pairs={{0,6},{1,7},{2,0},{3,1},{4,2},{5,3},{6,4},{7,5},{8,14},{9,15},{10,... | collective-permute-start | bytes 294920 | tf_op jit(solution)/shard_map/ppermute | solution.py:30
  362.4 35.2 %collective-permute-start.51 = (bf16[192,2048]{1,0:T(8,128)(2,1)S(1)}, bf16[192,2048]{1,0:T(8,128)(2,1)S(1)}, u32[]{:S(2)}, u32[]{:S(2)}) collective-permute-start(bf16[192,2048]{1,0:T(8,128)(2,1)S(1)} %slice.244), channel_id=1, source_target_pairs={{0,8},{8,0},{16,24},{24,16},{1,9},{9,1},{17,25},{25,17},{2,10},{10... | collective-permute-start | bytes 2359304 | tf_op jit(solution)/shard_map/ppermute | solution.py:13
  379.6 25.3 %collective-permute-start.52 = (bf16[192,2048]{1,0:T(8,128)(2,1)S(1)}, bf16[192,2048]{1,0:T(8,128)(2,1)S(1)}, u32[]{:S(2)}, u32[]{:S(2)}) collective-permute-start(bf16[192,2048]{1,0:T(8,128)(2,1)S(1)} %slice.245), channel_id=1, source_target_pairs={{0,16},{8,24},{16,0},{24,8},{1,17},{9,25},{17,1},{25,9},{2,18},{10... | collective-permute-start | bytes 2359304 | tf_op jit(solution)/shard_map/ppermute | solution.py:13
  383.6 27.4 %collective-permute-start.53 = (bf16[192,2048]{1,0:T(8,128)(2,1)S(1)}, bf16[192,2048]{1,0:T(8,128)(2,1)S(1)}, u32[]{:S(2)}, u32[]{:S(2)}) collective-permute-start(bf16[192,2048]{1,0:T(8,128)(2,1)S(1)} %slice.246), channel_id=1, source_target_pairs={{0,8},{8,0},{16,24},{24,16},{1,9},{9,1},{17,25},{25,17},{2,10},{10... | collective-permute-start | bytes 2359304 | tf_op jit(solution)/shard_map/ppermute | solution.py:13
  387.0 25.7 %collective-permute-start.54 = (bf16[192,2048]{1,0:T(8,128)(2,1)S(1)}, bf16[192,2048]{1,0:T(8,128)(2,1)S(1)}, u32[]{:S(2)}, u32[]{:S(2)}) collective-permute-start(bf16[192,2048]{1,0:T(8,128)(2,1)S(1)} %slice.247), channel_id=1, source_target_pairs={{0,16},{8,24},{16,0},{24,8},{1,17},{9,25},{17,1},{25,9},{2,18},{10... | collective-permute-start | bytes 2359304 | tf_op jit(solution)/shard_map/ppermute | solution.py:13
  387.3 25.5 %collective-permute-start.47 = (bf16[2,384,512]{2,1,0:T(8,128)(2,1)S(1)}, bf16[2,384,512]{2,1,0:T(8,128)(2,1)S(1)}, u32[]{:S(2)}, u32[]{:S(2)}) collective-permute-start(bf16[2,384,512]{2,1,0:T(8,128)(2,1)S(1)} %fusion.36), channel_id=1, source_target_pairs={{0,1},{1,0},{2,3},{3,2},{4,5},{5,4},{6,7},{7,6},{8,9},{9,8},{10,11... | collective-permute-start | bytes 2359304 | tf_op jit(solution)/shard_map/ppermute | solution.py:35
  397.6 32.5 %collective-permute-start.41 = (bf16[1,384,128]{2,1,0:T(8,128)(2,1)S(1)}, bf16[1,384,128]{2,1,0:T(8,128)(2,1)S(1)}, u32[]{:S(2)}, u32[]{:S(2)}) collective-permute-start(bf16[1,384,128]{2,1,0:T(8,128)(2,1)S(1)} %get-tuple-element.98), channel_id=1, source_target_pairs={{0,4},{1,5},{2,6},{3,7},{4,0},{5,1},{6,2},{7,3},{8,12},{9,13},{10,... | collective-permute-start | bytes 294920 | tf_op jit(solution)/shard_map/ppermute | solution.py:30
  413.3 21.9 %collective-permute-start.49 = (bf16[2,384,128]{2,1,0:T(8,128)(2,1)S(1)}, bf16[2,384,128]{2,1,0:T(8,128)(2,1)S(1)}, u32[]{:S(2)}, u32[]{:S(2)}) collective-permute-start(bf16[2,384,128]{2,1,0:T(8,128)(2,1)S(1)} %get-tuple-element.89), channel_id=1, source_target_pairs={{0,4},{1,5},{2,6},{3,7},{4,0},{5,1},{6,2},{7,3},{8,12},{9,13},{10,... | collective-permute-start | bytes 589832 | tf_op jit(solution)/shard_map/ppermute | solution.py:30
  421.0 12.1 %collective-permute-start.48 = (bf16[2,384,128]{2,1,0:T(8,128)(2,1)S(1)}, bf16[2,384,128]{2,1,0:T(8,128)(2,1)S(1)}, u32[]{:S(2)}, u32[]{:S(2)}) collective-permute-start(bf16[2,384,128]{2,1,0:T(8,128)(2,1)S(1)} %get-tuple-element.90), channel_id=1, source_target_pairs={{0,2},{1,3},{2,4},{3,5},{4,6},{5,7},{6,0},{7,1},{8,10},{9,11},{10,... | collective-permute-start | bytes 589832 | tf_op jit(solution)/shard_map/ppermute | solution.py:30
  425.9 9.2 %collective-permute-start.50 = (bf16[2,384,128]{2,1,0:T(8,128)(2,1)S(1)}, bf16[2,384,128]{2,1,0:T(8,128)(2,1)S(1)}, u32[]{:S(2)}, u32[]{:S(2)}) collective-permute-start(bf16[2,384,128]{2,1,0:T(8,128)(2,1)S(1)} %get-tuple-element.88), channel_id=1, source_target_pairs={{0,6},{1,7},{2,0},{3,1},{4,2},{5,3},{6,4},{7,5},{8,14},{9,15},{10,... | collective-permute-start | bytes 589832 | tf_op jit(solution)/shard_map/ppermute | solution.py:30
  430.0 5.2 %collective-permute-start.55 = (bf16[1,384,512]{2,1,0:T(8,128)(2,1)S(1)}, bf16[1,384,512]{2,1,0:T(8,128)(2,1)S(1)}, u32[]{:S(2)}, u32[]{:S(2)}) collective-permute-start(bf16[1,384,512]{2,1,0:T(8,128)(2,1)S(1)} %dynamic-slice_bitcast_fusion), channel_id=1, source_target_pairs={{0,1},{1,0},{2,3},{3,2},{4,5},{5,4},{6,7},{7,6},{8,9},{9,8},{10,11... | collective-permute-start | bytes 1179656 | tf_op jit(solution)/shard_map/ppermute | solution.py:35
  435.5 10.9 %collective-permute-start.57 = (bf16[1,384,128]{2,1,0:T(8,128)(2,1)S(1)}, bf16[1,384,128]{2,1,0:T(8,128)(2,1)S(1)}, u32[]{:S(2)}, u32[]{:S(2)}) collective-permute-start(bf16[1,384,128]{2,1,0:T(8,128)(2,1)S(1)} %get-tuple-element.102), channel_id=1, source_target_pairs={{0,4},{1,5},{2,6},{3,7},{4,0},{5,1},{6,2},{7,3},{8,12},{9,13},{10,... | collective-permute-start | bytes 294920 | tf_op jit(solution)/shard_map/ppermute | solution.py:30
  439.8 6.5 %collective-permute-start.56 = (bf16[1,384,128]{2,1,0:T(8,128)(2,1)S(1)}, bf16[1,384,128]{2,1,0:T(8,128)(2,1)S(1)}, u32[]{:S(2)}, u32[]{:S(2)}) collective-permute-start(bf16[1,384,128]{2,1,0:T(8,128)(2,1)S(1)} %get-tuple-element.103), channel_id=1, source_target_pairs={{0,2},{1,3},{2,4},{3,5},{4,6},{5,7},{6,0},{7,1},{8,10},{9,11},{10,... | collective-permute-start | bytes 294920 | tf_op jit(solution)/shard_map/ppermute | solution.py:30
  439.8 6.5 %collective-permute-start.58 = (bf16[1,384,128]{2,1,0:T(8,128)(2,1)S(1)}, bf16[1,384,128]{2,1,0:T(8,128)(2,1)S(1)}, u32[]{:S(2)}, u32[]{:S(2)}) collective-permute-start(bf16[1,384,128]{2,1,0:T(8,128)(2,1)S(1)} %get-tuple-element.101), channel_id=1, source_target_pairs={{0,6},{1,7},{2,0},{3,1},{4,2},{5,3},{6,4},{7,5},{8,14},{9,15},{10,... | collective-permute-start | bytes 294920 | tf_op jit(solution)/shard_map/ppermute | solution.py:30
  451.2 14.4 %all-to-all-start = ((bf16[4,576,128]{2,1,0:T(8,128)(2,1)}), bf16[4,576,128]{2,1,0:T(8,128)(2,1)}, u32[]{:S(2)}, u32[]{:S(2)}) async-start(bf16[4,576,128]{2,1,0:T(8,128)(2,1)} %fusion.40), calls=%async_computation | async-start | bytes 1179648 | tf_op jit(solution)/shard_map/all_to_all | solution.py:150
  466.7 14.6 %collective-permute-start.59 = (bf16[576,128]{1,0:T(8,128)(2,1)S(1)}, bf16[576,128]{1,0:T(8,128)(2,1)S(1)}, u32[]{:S(2)}, u32[]{:S(2)}) collective-permute-start(bf16[576,128]{1,0:T(8,128)(2,1)S(1)} %get-tuple-element.96), channel_id=1, source_target_pairs={{0,6},{1,7},{2,0},{3,1},{4,2},{5,3},{6,4},{7,5},{8,14},{9,15},{10,... | collective-permute-start | bytes 442376 | tf_op jit(solution)/shard_map/ppermute | solution.py:30
  470.4 10.8 %collective-permute-start.60 = (bf16[576,128]{1,0:T(8,128)(2,1)S(1)}, bf16[576,128]{1,0:T(8,128)(2,1)S(1)}, u32[]{:S(2)}, u32[]{:S(2)}) collective-permute-start(bf16[576,128]{1,0:T(8,128)(2,1)S(1)} %get-tuple-element.95), channel_id=1, source_target_pairs={{0,4},{1,5},{2,6},{3,7},{4,0},{5,1},{6,2},{7,3},{8,12},{9,13},{10,... | collective-permute-start | bytes 442376 | tf_op jit(solution)/shard_map/ppermute | solution.py:30
  470.4 10.8 %collective-permute-start.61 = (bf16[576,128]{1,0:T(8,128)(2,1)S(1)}, bf16[576,128]{1,0:T(8,128)(2,1)S(1)}, u32[]{:S(2)}, u32[]{:S(2)}) collective-permute-start(bf16[576,128]{1,0:T(8,128)(2,1)S(1)} %get-tuple-element.94), channel_id=1, source_target_pairs={{0,2},{1,3},{2,4},{3,5},{4,6},{5,7},{6,0},{7,1},{8,10},{9,11},{10,... | collective-permute-start | bytes 442376 | tf_op jit(solution)/shard_map/ppermute | solution.py:30
  (26 other events, 177.8 us)
